TPU v7x, 32 devices: a whole 2x2x4 slice. The times are simulated.
32 devices in a mesh: dp: 4 (over y, x), mp: 8 (over z, core).
Axes of the slice: x: 2, y: 2, z: 4, core: 2. Of those that a mesh axis runs over, the one named last changes fastest.
Arguments:
- grad: bfloat16 [4096, 8192], P(('dp', 'mp')), as said below
- block_owner: int32 [32], replicated, may hold values from 0 to 31, as said below
- left_stat: float32 [32, 1024, 1024], P(('dp', 'mp')), as said below
- right_stat: float32 [32, 1024, 1024], P(('dp', 'mp')), as said below
- left_root: bfloat16 [32, 1024, 1024], P(('dp', 'mp'))
- right_root: bfloat16 [32, 1024, 1024], P(('dp', 'mp'))
Outputs:
- new_left: float32 [32, 1024, 1024], P(('dp', 'mp'))
- new_right: float32 [32, 1024, 1024], P(('dp', 'mp'))
- update: bfloat16 [4096, 8192], P(('dp', 'mp'))
Inputs may be any that keep to these rules, and one draw needn't show every extreme that they name: `block_owner`: A permutation: each device owns exactly one block, and of each band's 8 blocks exactly 2 are owned by devices of each dp index (owner = dp index * 8 + mp index). `grad`: gradient entries, scaled per row and per column. `left_stat`: symmetric positive definite. `right_stat`: symmetric positive definite.
All inputs are finite; a program needn't handle non-finite values.
Results may differ from a plain program's by a relative error of at most 0.0039.
The roundings to bfloat16 on the way count: a program that leaves them out, or rounds other values in their place, can miss the bound.
Values may be sent and summed in bfloat16 or wider, within the bound.
No kernel may reach another device: no remote copies, remote signals or barrier semaphores. Data moves between devices by JAX's collectives and lax.ppermute only.
A program may use at most 256 MiB of HBM per device.

v0:
```python
import jax
import jax.numpy as jnp
from jax import lax
from jax.sharding import PartitionSpec as P

BLK = 1024


clip_level = 0.5
beta_stat = 0.95


def per_device(grad, block_owner, left_stat, right_stat, left_root, right_root):
    dp_count = lax.axis_size("dp")
    mp_count = lax.axis_size("mp")
    devices = dp_count * mp_count
    group_size = mp_count // dp_count
    my_band = lax.axis_index("dp")
    shard_rows = grad.shape[0]
    shard_cols = grad.shape[1]
    table = block_owner.reshape(dp_count, mp_count)
    band_owners = lax.dynamic_index_in_dim(table, my_band, 0, keepdims=False)
    pieces = grad.reshape(shard_rows, mp_count, BLK)
    column_order = jnp.argsort(band_owners)
    outbound = jnp.take(pieces, column_order, axis=1)
    banded = lax.all_to_all(outbound, "dp", split_axis=1, concat_axis=1, tiled=True)
    sorted_owners = jnp.sort(table, axis=1)
    local_owners = lax.dynamic_slice_in_dim(
        sorted_owners, my_band * group_size, group_size, 1
    ).reshape(mp_count)
    owner_cols = local_owners % mp_count
    sectioned = jnp.take(banded, jnp.argsort(owner_cols), axis=1)
    arrived = lax.all_to_all(sectioned, "mp", split_axis=1, concat_axis=0, tiled=True)
    block = arrived.reshape(BLK, BLK)
    values = block.astype(jnp.float32)
    total = lax.psum(jnp.sum(values * values), ("dp", "mp"))
    mean_square = total / (shard_rows * shard_cols * devices)
    scale = clip_level / jnp.sqrt(mean_square + 1e-06)
    left_gram = jnp.dot(block, block.T, preferred_element_type=jnp.float32)
    right_gram = jnp.dot(block.T, block, preferred_element_type=jnp.float32)
    factor = (1.0 - beta_stat) * scale * scale / BLK
    left_new = beta_stat * left_stat[0] + factor * left_gram
    right_new = beta_stat * right_stat[0] + factor * right_gram
    partial_left = jnp.dot(left_root[0], block, preferred_element_type=jnp.float32).astype(
        jnp.bfloat16
    )
    update_block = (
        jnp.dot(partial_left, right_root[0], preferred_element_type=jnp.float32) * scale
    ).astype(jnp.bfloat16)
    first_back = lax.all_to_all(
        update_block.reshape(BLK, 1, BLK), "mp", split_axis=0, concat_axis=1, tiled=True
    )
    second_send = jnp.take(first_back, owner_cols, axis=1)
    second_back = lax.all_to_all(second_send, "dp", split_axis=1, concat_axis=1, tiled=True)
    mine = jnp.take(second_back, jnp.argsort(column_order), axis=1)
    update = mine.reshape(shard_rows, shard_cols)
    return (left_new[None], right_new[None], update)


def solution(mesh):
    in_specs = (
        P(("dp", "mp"), None),
        P(),
        P(("dp", "mp"), None, None),
        P(("dp", "mp"), None, None),
        P(("dp", "mp"), None, None),
        P(("dp", "mp"), None, None),
    )
    out_specs = (P(("dp", "mp"), None, None), P(("dp", "mp"), None, None), P(("dp", "mp"), None))
    return jax.shard_map(
        per_device, mesh=mesh, in_specs=in_specs, out_specs=out_specs, check_vma=False
    )
```

profile of v0, /device:TPU:0, one launch (start us, length us, event | category | flops | bytes accessed | tf_op | source)
XLA Modules:
  0.0 273.7 jit_solution(3240310677695628443)
XLA Ops:
  1.6 1.0 sort.60
  3.5 4.1 %copy.36 = bf16[128,8192]{0,1:T(8,128)(2,1)} copy(bf16[128,8192]{1,0:T(8,128)(2,1)} %param.8) | data formatting | bytes 4194304 | tf_op args[0]
  7.5 3.9 %copy.37 = bf16[128,8,1024]{2,0,1:T(8,128)(2,1)} copy(bf16[128,8,1024]{0,2,1:T(8,128)(2,1)} %bitcast.64) | data formatting | bytes 4194304 | tf_op jit(solution)/shard_map/reshape | solution.py:23
  11.5 3.6 %gather_fusion = bf16[8,128,1024]{2,1,0:T(8,128)(2,1)} fusion(bf16[128,8,1024]{2,0,1:T(8,128)(2,1)} %copy.37, s32[1024]{0:T(1024)S(1)} %pad_clamp_fusion.3), kind=kCustom, calls=%fused_computation.clone | custom fusion | bytes 4194336 | tf_op jit(solution)/shard_map/jit(_take)/gather | solution.py:25
  15.0 3.2 %select_bitcast_fusion.3 = bf16[128,8,1024]{2,0,1:T(8,128)(2,1)} fusion(bf16[8,128,1024]{2,1,0:T(8,128)(2,1)} %gather_fusion, pred[8]{0:T(512)(128)(4,1)S(1)} %get-tuple-element.18), kind=kLoop, calls=%fused_computation.18 | loop fusion | flops 1048576 | bytes 4194312 | tf_op jit(solution)/shard_map/jit(_take)/select_n | solution.py:25
  18.2 5.2 %all-to-all-start = ((bf16[128,8,1024]{2,0,1:T(8,128)(2,1)}), bf16[128,8,1024]{2,0,1:T(8,128)(2,1)}, u32[]{:S(2)}, u32[]{:S(2)}) async-start(bf16[128,8,1024]{2,0,1:T(8,128)(2,1)} %select_bitcast_fusion.3), calls=%async_computation | async-start | bytes 4194304 | tf_op jit(solution)/shard_map/all_to_all | solution.py:26
  23.4 1.0 sort.62
  24.4 24.7 %all-to-all-done = bf16[128,8,1024]{2,0,1:T(8,128)(2,1)} async-done(((bf16[128,8,1024]{2,0,1:T(8,128)(2,1)}), bf16[128,8,1024]{2,0,1:T(8,128)(2,1)}, u32[]{:S(2)}, u32[]{:S(2)}) %all-to-all-start) | async-done | bytes 2097184 | tf_op jit(solution)/shard_map/all_to_all | solution.py:26
  49.1 3.6 %gather_fusion.1 = bf16[8,128,1024]{2,1,0:T(8,128)(2,1)} fusion(bf16[128,8,1024]{2,0,1:T(8,128)(2,1)} %all-to-all-done, s32[1024]{0:T(1024)S(1)} %pad_clamp_fusion.2), kind=kCustom, calls=%fused_computation.1.clone | custom fusion | bytes 4194336 | tf_op jit(solution)/shard_map/jit(_take)/gather | solution.py:32
  52.7 1.9 select_bitcast_fusion.2
  54.6 53.9 %all_to_all.43 = bf16[128,8,1024]{2,0,1:T(8,128)(2,1)S(1)} all-to-all(bf16[128,8,1024]{2,0,1:T(8,128)(2,1)S(1)} %select_bitcast_fusion.2), channel_id=1, replica_groups=mesh['dp'=4,'mp'=8] {'mp'}, dimensions={1} | all-to-all | bytes 4194304 | tf_op jit(solution)/shard_map/all_to_all | solution.py:33
  108.5 1.3 copy-done.2
  109.8 1.7 multiply_reduce_fusion
  111.5 37.6 %psum.7 = f32[]{:T(128)} all-reduce(f32[]{:T(128)} %multiply_reduce_fusion), channel_id=1, replica_groups=mesh['dp'=4,'mp'=8] {'dp','mp'}, use_global_device_ids=true, to_apply=%region_4.6 | all-reduce | flops 1 | bytes 8 | tf_op jit(solution)/shard_map/psum | solution.py:36
  149.8 8.1 %fusion.8 = bf16[1024,1,1024]{2,0,1:T(8,128)(2,1)} fusion(f32[]{:T(128)S(6)} %div.11, bf16[1,1024,1024]{2,1,0:T(8,128)(2,1)S(1)} %copy-done, bf16[1024,1024]{1,0:T(8,128)(2,1)} %bitcast.61, bf16[1,1024,1024]{2,1,0:T(8,128)(2,1)} %param.12), kind=kOutput, calls=%fused_computation.20 | convolution fusion | flops 4298113024 | bytes 8388612 | tf_op jit(solution)/shard_map/dot_general | solution.py:48
  158.4 3.9 %reduce.1 = bf16[1024,1024]{1,0:T(8,128)(2,1)S(1)} reduce(bf16[1024,1,1024]{2,0,1:T(8,128)(2,1)} %fusion.8, bf16[]{:T(256)} %broadcast.112), dimensions={1}, to_apply=%copy.39.reduce_sub_computation | reduce | bytes 4194306 | tf_op jit(solution)/shard_map/reshape | solution.py:51
  162.3 3.8 %reshape.90 = bf16[8,2,65536]{2,1,0:T(2,128)(2,1)} reshape(bf16[1024,1024]{1,0:T(8,128)(2,1)S(1)} %reduce.1) | data formatting | bytes 4194304
  166.1 3.7 %all-to-all-start.2 = ((bf16[8,2,65536]{2,1,0:T(2,128)(2,1)}), bf16[8,2,65536]{2,1,0:T(2,128)(2,1)S(1)}, u32[]{:S(2)}, u32[]{:S(2)}) async-start(bf16[8,2,65536]{2,1,0:T(2,128)(2,1)} %reshape.90), calls=%async_computation.2 | async-start | bytes 4194304 | tf_op jit(solution)/shard_map/all_to_all | solution.py:50
  169.8 1.0 sort.63
  170.8 48.0 %all-to-all-done.2 = bf16[8,2,65536]{2,1,0:T(2,128)(2,1)S(1)} async-done(((bf16[8,2,65536]{2,1,0:T(2,128)(2,1)}), bf16[8,2,65536]{2,1,0:T(2,128)(2,1)S(1)}, u32[]{:S(2)}, u32[]{:S(2)}) %all-to-all-start.2) | async-done | bytes 2097184 | tf_op jit(solution)/shard_map/all_to_all | solution.py:50
  218.8 4.3 %reshape.91 = bf16[1024,1,1024]{2,1,0:T(2,128)(2,1)} reshape(bf16[8,2,65536]{2,1,0:T(2,128)(2,1)S(1)} %all-to-all-done.2) | data formatting | bytes 4194304
  223.2 3.0 %copy.43 = bf16[1024,1,1024]{2,0,1:T(8,128)(2,1)S(1)} copy(bf16[1024,1,1024]{2,1,0:T(2,128)(2,1)} %reshape.91) | data formatting | bytes 4194304
  226.2 2.0 gather_fusion.2
  228.2 3.1 %select_bitcast_fusion.1 = bf16[128,8,1024]{2,0,1:T(8,128)(2,1)} fusion(bf16[8,128,1024]{2,1,0:T(8,128)(2,1)} %gather_fusion.2, pred[8]{0:T(512)(128)(4,1)S(1)} %get-tuple-element.16), kind=kLoop, calls=%fused_computation.16 | loop fusion | flops 1048576 | bytes 4194312 | tf_op jit(solution)/shard_map/jit(_take)/select_n | solution.py:53
  231.3 4.8 %all-to-all-start.3 = ((bf16[128,8,1024]{2,0,1:T(8,128)(2,1)}), bf16[128,8,1024]{2,0,1:T(8,128)(2,1)}, u32[]{:S(2)}, u32[]{:S(2)}) async-start(bf16[128,8,1024]{2,0,1:T(8,128)(2,1)} %select_bitcast_fusion.1), calls=%async_computation.3 | async-start | bytes 4194304 | tf_op jit(solution)/shard_map/all_to_all | solution.py:54
  236.1 6.8 %fusion.1 = f32[1,1024,1024]{2,1,0:T(8,128)} fusion(f32[1,1024,1024]{2,1,0:T(8,128)} %param.11, bf16[128,8,1024]{2,0,1:T(8,128)(2,1)S(1)} %copy-done.3, f32[]{:T(128)S(6)} %div.10), kind=kOutput, calls=%fused_computation.6 | convolution fusion | flops 2150629376 | bytes 10485764 | tf_op jit(solution)/shard_map/dot_general | solution.py:40
  242.9 4.4 %fusion.2 = f32[1,1024,1024]{2,1,0:T(8,128)} fusion(f32[1,1024,1024]{2,1,0:T(8,128)S(1)} %copy-done.4, bf16[1024,1024]{1,0:T(8,128)(2,1)S(1)} %bitcast.62, f32[]{:T(128)S(6)} %div.10), kind=kOutput, calls=%fused_computation.8 | convolution fusion | flops 2150629376 | bytes 10485764 | tf_op jit(solution)/shard_map/dot_general | solution.py:39
  247.3 14.4 %all-to-all-done.3 = bf16[128,8,1024]{2,0,1:T(8,128)(2,1)} async-done(((bf16[128,8,1024]{2,0,1:T(8,128)(2,1)}), bf16[128,8,1024]{2,0,1:T(8,128)(2,1)}, u32[]{:S(2)}, u32[]{:S(2)}) %all-to-all-start.3) | async-done | bytes 2097184 | tf_op jit(solution)/shard_map/all_to_all | solution.py:54
  261.7 2.3 gather_fusion.3
  264.0 1.6 select_bitcast_fusion
  265.6 3.9 %copy.40 = bf16[128,8,1024]{0,2,1:T(8,128)(2,1)} copy(bf16[128,8,1024]{2,0,1:T(8,128)(2,1)} %select_bitcast_fusion) | data formatting | bytes 4194304 | tf_op jit(solution)/shard_map/jit(_take)/select_n | solution.py:55
  269.5 4.2 %copy.41 = bf16[128,8192]{1,0:T(8,128)(2,1)} copy(bf16[128,8192]{0,1:T(8,128)(2,1)} %bitcast.63) | data formatting | bytes 4194304
  (32 shorter events, 2.4 us)
Async XLA Ops:
  0.6 149.1 %copy-start = (bf16[1,1024,1024]{2,1,0:T(8,128)(2,1)S(1)}, bf16[1,1024,1024]{2,1,0:T(8,128)(2,1)}, u32[]{:S(2)}) copy-start(bf16[1,1024,1024]{2,1,0:T(8,128)(2,1)} %param.13) | copy-start | bytes 6291460
  18.2 30.9 %all-to-all-start = ((bf16[128,8,1024]{2,0,1:T(8,128)(2,1)}), bf16[128,8,1024]{2,0,1:T(8,128)(2,1)}, u32[]{:S(2)}, u32[]{:S(2)}) async-start(bf16[128,8,1024]{2,0,1:T(8,128)(2,1)} %select_bitcast_fusion.3), calls=%async_computation | async-start | bytes 4194304 | tf_op jit(solution)/shard_map/all_to_all | solution.py:26
  108.5 1.3 copy-start.2
  166.1 52.7 %all-to-all-start.2 = ((bf16[8,2,65536]{2,1,0:T(2,128)(2,1)}), bf16[8,2,65536]{2,1,0:T(2,128)(2,1)S(1)}, u32[]{:S(2)}, u32[]{:S(2)}) async-start(bf16[8,2,65536]{2,1,0:T(2,128)(2,1)} %reshape.90), calls=%async_computation.2 | async-start | bytes 4194304 | tf_op jit(solution)/shard_map/all_to_all | solution.py:50
  231.3 4.8 %copy-start.3 = (bf16[128,8,1024]{2,0,1:T(8,128)(2,1)S(1)}, bf16[128,8,1024]{2,0,1:T(8,128)(2,1)}, u32[]{:S(2)}) copy-start(bf16[128,8,1024]{2,0,1:T(8,128)(2,1)} %copy-done.2) | copy-start | bytes 6291460
  231.3 30.4 %all-to-all-start.3 = ((bf16[128,8,1024]{2,0,1:T(8,128)(2,1)}), bf16[128,8,1024]{2,0,1:T(8,128)(2,1)}, u32[]{:S(2)}, u32[]{:S(2)}) async-start(bf16[128,8,1024]{2,0,1:T(8,128)(2,1)} %select_bitcast_fusion.1), calls=%async_computation.3 | async-start | bytes 4194304 | tf_op jit(solution)/shard_map/all_to_all | solution.py:54
  236.1 6.8 %copy-start.4 = (f32[1,1024,1024]{2,1,0:T(8,128)S(1)}, f32[1,1024,1024]{2,1,0:T(8,128)}, u32[]{:S(2)}) copy-start(f32[1,1024,1024]{2,1,0:T(8,128)} %param.10) | copy-start | bytes 12582916
  269.5 4.2 %copy-start.1 = (bf16[1,1024,1024]{2,1,0:T(8,128)(2,1)S(1)}, bf16[1,1024,1024]{2,1,0:T(8,128)(2,1)}, u32[]{:S(2)}) copy-start(bf16[1,1024,1024]{2,1,0:T(8,128)(2,1)} %param.13) | copy-start | bytes 6291460
where the time goes:
time: 275 us; the launch traced here: 274 us
  blocking collectives  91.5 us (33%)
  waiting for transfers between devices  87.2 us (32%)
  local copies, waits for them, and re-layouts  41.7 us (15%)
  matrix products  19.3 us (7%)
  other arithmetic  19 us (7%)
  starting transfers between devices  13.7 us (5%)
    all_to_all x1, blocking collectives, per_device(): lax.all_to_all(sectioned, 'mp', split_axis=1, concat_axis=0, tiled=True)  53.9 us
    all_to_all x1, waiting for transfers between devices, per_device(): lax.all_to_all(update_block.reshape(BLK, 1, BLK), 'mp', split_axis=0, con...  48 us
    psum x1, blocking collectives, per_device(): total = lax.psum(jnp.sum(values * values), ('dp', 'mp'))  37.6 us
    all_to_all x1, waiting for transfers between devices, per_device(): lax.all_to_all(outbound, 'dp', split_axis=1, concat_axis=1, tiled=True)  24.7 us
    unnamed x15, local copies, waits for them, and re-layouts  20.7 us
    all_to_all x1, waiting for transfers between devices, per_device(): lax.all_to_all(second_send, 'dp', split_axis=1, concat_axis=1, tiled=True)  14.4 us
    dot_general x1, matrix products, per_device(): jnp.dot(partial_left, right_root[0], preferred_element_type=jnp.float32)  8.13 us
    dot_general x1, matrix products, per_device(): right_gram = jnp.dot(block.T, block, preferred_element_type=jnp.float32)  6.77 us
  transfers between devices with their start and end apart: 3, of which 3 were waited for; matrix products, arithmetic and copies ran while one was open for 5% of the time, Pallas kernels for 0%

commit v1 on v0

v1 whole, which is shorter than its diff:
```python
import jax
import jax.numpy as jnp
from jax import lax
from jax.experimental import pallas as pl
from jax.experimental.pallas import tpu as pltpu
from jax.sharding import PartitionSpec as P


clip_level = 0.5
beta_stat = 0.95

FORWARD = (3, 5)
BACKWARD = (3, 3, 2)
ANY = pl.BlockSpec(memory_space=pl.ANY)
SMEM = pl.BlockSpec(memory_space=pltpu.SMEM)
VMEM = pl.BlockSpec(memory_space=pltpu.VMEM)
HBM = pl.BlockSpec(memory_space=pltpu.HBM)


def spans(parts, size):
    total, at, out = sum(parts), 0, []
    for part in parts:
        out.append((at * size // total, part * size // total))
        at += part
    return out


def band_columns(owner, band, target, mp, group):
    count = jnp.int32(0)
    columns = [jnp.int32(0)] * group
    for c in range(mp):
        match = owner[band * mp + c] // mp == target
        for j in range(group):
            columns[j] = jnp.where(match & (count == j), c, columns[j])
        count = count + match.astype(jnp.int32)
    return columns


def call(body, outs, inputs, owner, scratch=(), ins=VMEM, out=VMEM, aliases=None, flops=0, mib=8):
    ins = ins if isinstance(ins, list) else [ins] * len(inputs)
    return pl.pallas_call(
        body,
        out_shape=outs,
        in_specs=[SMEM] + ins,
        out_specs=[out] * len(outs),
        scratch_shapes=list(scratch),
        input_output_aliases=aliases or {},
        cost_estimate=pl.CostEstimate(flops=flops, bytes_accessed=1 << 21, transcendentals=0),
        compiler_params=pltpu.CompilerParams(vmem_limit_bytes=mib << 20),
    )(owner, *inputs)


def pack(grad, owner, dp, mp, blk, cuts):
    rows = grad.shape[0]
    group = mp // dp

    def body(owner, grad, *rest):
        outs, sems = rest[:-1], rest[-1]
        me = lax.axis_index("dp")
        copies = []
        for k in list(range(1, dp)) + [0]:
            columns = band_columns(owner, me, me ^ k, mp, group)
            for j in range(group):
                for c, (at, width) in enumerate(cuts):
                    start = pl.multiple_of(columns[j] * blk + at, 128)
                    copy = pltpu.make_async_copy(
                        grad.at[:, pl.ds(start, width)],
                        outs[c * dp + k].at[j],
                        sems.at[(c * dp + k) * group + j],
                    )
                    copy.start()
                    copies.append(copy)
        for copy in copies:
            copy.wait()

    outs = [jax.ShapeDtypeStruct((group, rows, width), grad.dtype) for _, width in cuts for _ in range(dp)]
    scratch = [pltpu.SemaphoreType.DMA((mp * len(cuts),))]
    grad = pltpu.with_memory_space_constraint(grad, pltpu.HBM)
    flat = call(body, outs, [grad], owner, scratch, ins=HBM)
    return [flat[c * dp : (c + 1) * dp] for c in range(len(cuts))]


def square_sum(grad, owner):
    rows, cols = grad.shape
    step = min(1024, cols)

    def body(owner, grad, out):
        total = jnp.zeros((8, step), jnp.float32)
        for i in range(cols // step):
            values = grad[:, i * step : (i + 1) * step].astype(jnp.float32)
            total = total + jnp.sum((values * values).reshape(rows // 8, 8, step), axis=0)
        out[...] = jnp.full(out.shape, jnp.sum(total), jnp.float32)

    return call(body, [jax.ShapeDtypeStruct((8, 128), jnp.float32)], [grad], owner)[0]


def fill_table(owner, table, me, dp, mp, group):
    for band in range(dp):
        count = jnp.int32(0)
        for c in range(mp):
            o = owner[band * mp + c]
            match = o // mp == me
            table[jnp.where(match, o % mp, mp)] = (band ^ me) * group + count
            count = count + match.astype(jnp.int32)


def route(got, owner, dp, mp):
    group, rows, width = got[0].shape

    def body(owner, *rest):
        got, outs, table = rest[:dp], rest[dp : dp + mp], rest[dp + mp]
        fill_table(owner, table, lax.axis_index("dp"), dp, mp, group)
        mine = lax.axis_index("mp")
        for kk in range(mp):
            entry = table[mine ^ kk]
            for k in range(dp):

                @pl.when(entry // group == k)
                def _(k=k, kk=kk, entry=entry):
                    outs[kk][...] = got[k][entry % group]

    outs = [jax.ShapeDtypeStruct((rows, width), got[0].dtype)] * mp
    return call(body, outs, got, owner, [pltpu.SMEM((mp + 1,), jnp.int32)])


def unroute(pieces, owner, dp, mp):
    rows, width = pieces[0].shape
    group = mp // dp

    def body(owner, *rest):
        pieces, outs, table = rest[:mp], rest[mp : mp + dp], rest[mp + dp]
        fill_table(owner, table, lax.axis_index("dp"), dp, mp, group)
        mine = lax.axis_index("mp")
        for kk in range(mp):
            entry = table[mine ^ kk]
            for k in range(dp):

                @pl.when(entry // group == k)
                def _(k=k, kk=kk, entry=entry):
                    outs[k][entry % group] = pieces[kk][...]

    outs = [jax.ShapeDtypeStruct((group, rows, width), pieces[0].dtype)] * dp
    return call(body, outs, list(pieces), owner, [pltpu.SMEM((mp + 1,), jnp.int32)])


def place(parts, owner, dp, mp, blk, cuts):
    group, rows = parts[0][0].shape[:2]
    count = len(cuts)

    def body(owner, *rest):
        parts, out, sems = rest[: count * dp], rest[-2], rest[-1]
        me = lax.axis_index("dp")
        copies = []
        for k in range(dp):
            columns = band_columns(owner, me, me ^ k, mp, group)
            for j in range(group):
                for c, (at, width) in enumerate(cuts):
                    start = pl.multiple_of(columns[j] * blk + at, 128)
                    copy = pltpu.make_async_copy(
                        parts[c * dp + k].at[j],
                        out.at[:, pl.ds(start, width)],
                        sems.at[(c * dp + k) * group + j],
                    )
                    copy.start()
                    copies.append(copy)
        for copy in copies:
            copy.wait()

    outs = [jax.ShapeDtypeStruct((rows, mp * blk), parts[0][0].dtype)]
    inputs = [part for chunk in parts for part in chunk]
    scratch = [pltpu.SemaphoreType.DMA((mp * count,))]
    return call(body, outs, inputs, owner, scratch, VMEM, ANY)[0]


def gather(pieces, block, mp, at, width):
    rows = pieces[0].shape[0]
    mine = lax.axis_index("mp")
    for kk in range(mp):
        start = pl.multiple_of((mine ^ kk) * rows, 16)
        block[pl.ds(start, rows), at : at + width] = pieces[kk][...]


def partial_update(pieces, left_root, right_root, old, owner, mp, at, width):
    blk = left_root.shape[0]
    tile = min(512, blk)

    def body(owner, *rest):
        pieces = rest[:mp]
        left, right = rest[mp : mp + 2]
        block, total = rest[-2:]
        gather(pieces, block, mp, at, width)

        @pl.loop(0, blk // tile)
        def _(i):
            span = pl.ds(pl.multiple_of(i * tile, tile), tile)
            half = jnp.dot(left[span, :], block[:, at : at + width], preferred_element_type=jnp.float32)
            term = jnp.dot(
                half.astype(block.dtype), right[at : at + width, :], preferred_element_type=jnp.float32
            )
            total[span, :] = term if old is None else total[span, :] + term

    outs = [
        jax.ShapeDtypeStruct((blk, blk), pieces[0].dtype),
        jax.ShapeDtypeStruct((blk, blk), jnp.float32),
    ]
    inputs = [*pieces, left_root, right_root, *(old or ())]
    aliases = None if old is None else {mp + 3: 0, mp + 4: 1}
    return call(body, outs, inputs, owner, aliases=aliases, flops=4 * blk * blk * width, mib=24)


def deal(update, outs, rows, mp, cuts):
    mine = lax.axis_index("mp")
    for c, (start, size) in enumerate(cuts):
        for kk in range(mp):
            row = pl.multiple_of((mine ^ kk) * rows, 16)
            outs[c * mp + kk][...] = update[pl.ds(row, rows), start : start + size]


def last_update(pieces, left_root, right_root, block, total, scale, owner, mp, at, width, cut):
    rows = pieces[0].shape[0]
    blk = left_root.shape[0]
    tile = min(512, blk)
    start, size = cut

    def body(owner, *rest):
        pieces = rest[:mp]
        left, right, total, scale, _, block, half = rest[mp : mp + 7]
        outs, update = rest[mp + 7 : -1], rest[-1]
        gather(pieces, block, mp, at, width)
        scaling = scale[0:1, 0:1]

        @pl.loop(0, blk // tile)
        def _(i):
            span = pl.ds(pl.multiple_of(i * tile, tile), tile)
            term = jnp.dot(left[span, :], block[:, at : at + width], preferred_element_type=jnp.float32)
            half[span, :] = term.astype(half.dtype)
            term = jnp.dot(
                term.astype(half.dtype),
                right[at : at + width, start : start + size],
                preferred_element_type=jnp.float32,
            )
            update[span, :] = ((total[span, start : start + size] + term) * scaling).astype(update.dtype)

        deal(update, outs, rows, mp, [(0, size)])

    dtype = pieces[0].dtype
    outs = [jax.ShapeDtypeStruct((blk, blk), dtype), jax.ShapeDtypeStruct((blk, width), dtype)]
    outs += [jax.ShapeDtypeStruct((rows, size), dtype)] * mp
    scratch = [pltpu.VMEM((blk, size), dtype)]
    inputs = [*pieces, left_root, right_root, total, scale, block]
    flops = 2 * blk * width * (blk + size)
    flat = call(body, outs, inputs, owner, scratch, aliases={mp + 5: 0}, flops=flops, mib=24)
    return flat[0], flat[1], flat[2:]


def rest_update(half, right_root, total, scale, rows, owner, mp, at, cuts):
    blk, width = half.shape
    tile = min(512, blk)
    base = cuts[0][0]

    def body(owner, half, right, total, scale, *rest):
        outs, update = rest[:-1], rest[-1]
        scaling = scale[0:1, 0:1]

        @pl.loop(0, blk // tile)
        def _(i):
            span = pl.ds(pl.multiple_of(i * tile, tile), tile)
            term = jnp.dot(half[span, :], right[at : at + width, base:], preferred_element_type=jnp.float32)
            update[span, :] = ((total[span, base:] + term) * scaling).astype(update.dtype)

        deal(update, outs, rows, mp, [(start - base, size) for start, size in cuts])

    outs = [jax.ShapeDtypeStruct((rows, size), half.dtype) for _, size in cuts for _ in range(mp)]
    scratch = [pltpu.VMEM((blk, blk - base), half.dtype)]
    flops = 2 * blk * width * (blk - base)
    flat = call(body, outs, [half, right_root, total, scale], owner, scratch, flops=flops, mib=24)
    return [flat[c * mp : (c + 1) * mp] for c in range(len(cuts))]


def swap(value, axis, distance):
    count = lax.axis_size(axis)
    return lax.ppermute(value, axis, [(i, i ^ distance) for i in range(count)])


def far_first(count):
    return list(range(count // 2, count)) + list(range(1, count // 2))


def steps(count):
    step = 1
    while step < count:
        yield step
        step *= 2


def per_device(grad, owner, left_stat, right_stat, left_root, right_root):
    dp, mp = lax.axis_size("dp"), lax.axis_size("mp")
    blk = left_root.shape[-1]
    left_root, right_root = left_root[0], right_root[0]
    forward, backward = spans(FORWARD, blk), spans(BACKWARD, blk)

    packed = pack(grad, owner, dp, mp, blk, forward)
    crossed = [[part if k == 0 else swap(part, "dp", k) for k, part in enumerate(chunk)] for chunk in packed]
    total = square_sum(grad, owner)
    total = total + swap(total, "mp", 1)
    terms = [swap(total, "mp", k) for k in range(2, mp, 2)]
    total = sum(terms, total)
    for step in steps(dp):
        total = total + swap(total, "dp", step)
    mean_square = total / (grad.size * dp * mp)
    scale = clip_level / jnp.sqrt(mean_square + 1e-06)

    arrived = []
    for c in range(len(forward)):
        pieces = route(crossed[c], owner, dp, mp)
        moved = list(pieces)
        for k in far_first(mp):
            moved[k] = swap(pieces[k], "mp", k)
        arrived.append(moved)

    state = None
    for c, (at, width) in enumerate(forward[:-1]):
        state = partial_update(arrived[c], left_root, right_root, state, owner, mp, at, width)
    at, width = forward[-1]
    rows = arrived[0][0].shape[0]
    block, half, first = last_update(
        arrived[-1], left_root, right_root, *state, scale, owner, mp, at, width, backward[0]
    )
    leaving = [first] + rest_update(half, right_root, state[1], scale, rows, owner, mp, at, backward[1:])

    parts = []
    for c in range(len(backward)):
        pieces = list(leaving[c])
        for k in far_first(mp):
            pieces[k] = swap(leaving[c][k], "mp", k)
        chunk = list(unroute(pieces, owner, dp, mp))
        for k in range(1, dp):
            chunk[k] = swap(chunk[k], "dp", k)
        parts.append(chunk)
    out = place(parts, owner, dp, mp, blk, backward)

    factor = ((1.0 - beta_stat) * scale * scale / blk)[0, 0]
    left_gram = jnp.dot(block, block.T, preferred_element_type=jnp.float32)
    left_new = beta_stat * left_stat[0] + factor * left_gram
    right_gram = jnp.dot(block.T, block, preferred_element_type=jnp.float32)
    right_new = beta_stat * right_stat[0] + factor * right_gram
    return (left_new[None], right_new[None], out)


def solution(mesh):
    split = P(("dp", "mp"), None, None)
    rows = P(("dp", "mp"), None)

    return jax.shard_map(
        per_device,
        mesh=mesh,
        in_specs=(rows, P(), split, split, split, split),
        out_specs=(split, split, rows),
        check_vma=False,
    )
```

time: 275 us -> 171 us (0.62)
  blocking collectives: 91.5 us -> 0 us
  starting transfers between devices: 13.7 us -> 75 us
  local copies, waits for them, and re-layouts: 41.7 us -> 2.92 us
  waiting for transfers between devices: 87.2 us -> 60.3 us
  Pallas kernels: 0 us -> 20.5 us
  other arithmetic: 19 us -> 0.02 us
  matrix products: 19.3 us -> 10.5 us
    all_to_all x3 -> x0, waiting for transfers between devices: 87.2 us -> none  [the longest x1 48 us: per_device(): lax.all_to_all(update_block.reshape(BLK, 1, BLK), 'mp', split_axis=0, con...]
    ppermute x0 -> x56, starting transfers between devices: none -> 75 us  [swap(): return lax.ppermute(value, axis, [(i, i ^ distance) for i in range(count)])]
    ppermute x0 -> x56, waiting for transfers between devices: none -> 60.3 us  [swap(): return lax.ppermute(value, axis, [(i, i ^ distance) for i in range(count)])]
    all_to_all x1 -> x0, blocking collectives: 53.9 us -> none  [per_device(): lax.all_to_all(sectioned, 'mp', split_axis=1, concat_axis=0, tiled=True)]
    psum x1 -> x0, blocking collectives: 37.6 us -> none  [per_device(): total = lax.psum(jnp.sum(values * values), ('dp', 'mp'))]
    pallas_call x0 -> x11, Pallas kernels: none -> 20.5 us  [call(): pl.pallas_call(body, out_shape=outs, in_specs=[SMEM] + ins, out_specs=[ou...]
    unnamed x15 -> x14, local copies, waits for them, and re-layouts: 20.7 us -> 2.41 us
    all_to_all x3 -> x0, starting transfers between devices: 13.7 us -> none  [the longest x1 5.19 us: per_device(): lax.all_to_all(outbound, 'dp', split_axis=1, concat_axis=1, tiled=True)]
  transfers between devices with their start and end apart: 3 -> 56, of which waited for: 3 -> 19; matrix products, arithmetic and copies ran while one was open for 5% -> 6% of each run, Pallas kernels for 0% -> 6%
where the time goes in v1:
time: 171 us; the launch traced here: 170 us
  starting transfers between devices  75 us (44%)
  waiting for transfers between devices  60.3 us (35%)
  Pallas kernels  20.5 us (12%)
  matrix products  10.5 us (6%)
  local copies, waits for them, and re-layouts  2.92 us (2%)
    ppermute x56, starting transfers between devices, swap(): return lax.ppermute(value, axis, [(i, i ^ distance) for i in range(count)])  75 us
    ppermute x56, waiting for transfers between devices, swap(): return lax.ppermute(value, axis, [(i, i ^ distance) for i in range(count)])  60.3 us
    pallas_call x11, Pallas kernels, call(): pl.pallas_call(body, out_shape=outs, in_specs=[SMEM] + ins, out_specs=[ou...  20.5 us
    dot_general x1, matrix products, per_device(): right_gram = jnp.dot(block.T, block, preferred_element_type=jnp.float32)  5.42 us
    dot_general x1, matrix products, per_device(): left_gram = jnp.dot(block, block.T, preferred_element_type=jnp.float32)  5.07 us
  transfers between devices with their start and end apart: 56, of which 19 were waited for; matrix products, arithmetic and copies ran while one was open for 6% of the time, Pallas kernels for 6%

profile of v1, /device:TPU:0, one launch (start us, length us, event | category | flops | bytes accessed | tf_op | source)
XLA Modules:
  0.0 170.3 jit_solution(14145397120863973509)
XLA Ops:
  1.4 2.4 %shard_map.86 = (bf16[2,128,384]{2,1,0:T(8,128)(2,1)S(1)}, bf16[2,128,384]{2,1,0:T(8,128)(2,1)S(1)}, bf16[2,128,384]{2,1,0:T(8,128)(2,1)S(1)}, bf16[2,128,384]{2...) custom-call(s32[32]{0:T(128)S(1)} %copy-done.3, ...), custom_call_target="tpu_custom_call" | custom-call | bytes 2097152 | tf_op jit(solution)/shard_map/pallas_call | solution.py:41
  3.9 3.0 %collective-permute-start.16 = (bf16[2,128,384]{2,1,0:T(8,128)(2,1)S(1)}, bf16[2,128,384]{2,1,0:T(8,128)(2,1)S(1)}, u32[]{:S(2)}, u32[]{:S(2)}) collective-permute-start(bf16[2,128,384]{2,1,0:T(8,128)(2,1)S(1)} %get-tuple-element.80), channel_id=1, source_target_pairs={{0,8},{8,0},{16,24},{24,16},{1,9},{9,1},{17,25},{25,17},{2,10},{10... | collective-permute-start | bytes 589832 | tf_op jit(solution)/shard_map/ppermute | solution.py:282
  12.0 4.1 %collective-permute-start.3 = (f32[8,128]{1,0:T(8,128)S(1)}, f32[8,128]{1,0:T(8,128)S(1)}, u32[]{:S(2)}, u32[]{:S(2)}) collective-permute-start(f32[8,128]{1,0:T(8,128)S(1)} %add.30), channel_id=1, source_target_pairs={{0,6},{1,7},{2,4},{3,5},{4,2},{5,3},{6,0},{7,1},{8,14},{9,15},{10,... | collective-permute-start | bytes 12296 | tf_op jit(solution)/shard_map/ppermute | solution.py:282
  21.7 3.4 %collective-permute-start.1 = (f32[8,128]{1,0:T(8,128)S(1)}, f32[8,128]{1,0:T(8,128)S(1)}, u32[]{:S(2)}, u32[]{:S(2)}) collective-permute-start(f32[8,128]{1,0:T(8,128)S(1)} %add.30), channel_id=1, source_target_pairs={{0,2},{1,3},{2,0},{3,1},{4,6},{5,7},{6,4},{7,5},{8,10},{9,11},{10,... | collective-permute-start | bytes 12296 | tf_op jit(solution)/shard_map/ppermute | solution.py:282
  27.2 5.6 %collective-permute-done.4 = f32[8,128]{1,0:T(8,128)S(1)} collective-permute-done((f32[8,128]{1,0:T(8,128)S(1)}, f32[8,128]{1,0:T(8,128)S(1)}, u32[]{:S(2)}, u32[]{:S(2)}) %collective-permute-start.4) | collective-permute-done | bytes 4128 | tf_op jit(solution)/shard_map/ppermute | solution.py:282
  38.4 3.0 %collective-permute-start.10 = (bf16[128,640]{1,0:T(8,128)(2,1)S(1)}, bf16[128,640]{1,0:T(8,128)(2,1)S(1)}, u32[]{:S(2)}, u32[]{:S(2)}) collective-permute-start(bf16[128,640]{1,0:T(8,128)(2,1)S(1)} %get-tuple-element.73), channel_id=1, source_target_pairs={{0,2},{1,3},{2,0},{3,1},{4,6},{5,7},{6,4},{7,5},{8,10},{9,11},{10,... | collective-permute-start | bytes 491528 | tf_op jit(solution)/shard_map/ppermute | solution.py:282
  41.4 2.5 %collective-permute-start.24 = (bf16[128,384]{1,0:T(8,128)(2,1)S(1)}, bf16[128,384]{1,0:T(8,128)(2,1)S(1)}, u32[]{:S(2)}, u32[]{:S(2)}) collective-permute-start(bf16[128,384]{1,0:T(8,128)(2,1)S(1)} %get-tuple-element.89), channel_id=1, source_target_pairs={{0,6},{1,7},{2,4},{3,5},{4,2},{5,3},{6,0},{7,1},{8,14},{9,15},{10,... | collective-permute-start | bytes 294920 | tf_op jit(solution)/shard_map/ppermute | solution.py:282
  44.8 8.5 %collective-permute-done.23.rest_5_ = bf16[128,384]{1,0:T(8,128)(2,1)S(1)} collective-permute-done((bf16[128,384]{1,0:T(8,128)(2,1)S(1)}, bf16[128,384]{1,0:T(8,128)(2,1)S(1)}, u32[]{:S(2)}, u32[]{:S(2)}) %collective-permute-start.23) | collective-permute-done | bytes 98336 | tf_op jit(solution)/shard_map/ppermute | solution.py:282
  53.3 2.8 %collective-permute-start.12 = (bf16[128,640]{1,0:T(8,128)(2,1)S(1)}, bf16[128,640]{1,0:T(8,128)(2,1)S(1)}, u32[]{:S(2)}, u32[]{:S(2)}) collective-permute-start(bf16[128,640]{1,0:T(8,128)(2,1)S(1)} %get-tuple-element.75), channel_id=1, source_target_pairs={{0,4},{1,5},{2,6},{3,7},{4,0},{5,1},{6,2},{7,3},{8,12},{9,13},{10,... | collective-permute-start | bytes 491528 | tf_op jit(solution)/shard_map/ppermute | solution.py:282
  57.3 3.7 %collective-permute-start.14 = (bf16[128,640]{1,0:T(8,128)(2,1)S(1)}, bf16[128,640]{1,0:T(8,128)(2,1)S(1)}, u32[]{:S(2)}, u32[]{:S(2)}) collective-permute-start(bf16[128,640]{1,0:T(8,128)(2,1)S(1)} %get-tuple-element.77), channel_id=1, source_target_pairs={{0,6},{1,7},{2,4},{3,5},{4,2},{5,3},{6,0},{7,1},{8,14},{9,15},{10,... | collective-permute-start | bytes 491528 | tf_op jit(solution)/shard_map/ppermute | solution.py:282
  61.1 3.2 %shard_map.89 = (bf16[1024,1024]{1,0:T(8,128)(2,1)S(1)}, f32[1024,1024]{1,0:T(8,128)S(1)}) custom-call(s32[32]{0:T(128)S(1)} %copy-done.4, bf16[128,384]{1,0:T(8,128)(2,1)S(1)} %get-tuple-element.83.rest_0_, bf16[128,384]{1,0:T(8,128)(2,1)S(1)} %collective-permute-done.19.rest_1_, bf16[128,384]{1,0:T(8,128)(2,1)S(1)} %collective-permute-done.20.rest_2_, ...), custom_call_target="tpu_custom_call" | custom-call | flops 1610612736 | bytes 2097152 | tf_op jit(solution)/shard_map/pallas_call | solution.py:41
  64.3 11.5 %collective-permute-done.12.rest_4_ = bf16[128,640]{1,0:T(8,128)(2,1)S(1)} collective-permute-done((bf16[128,640]{1,0:T(8,128)(2,1)S(1)}, bf16[128,640]{1,0:T(8,128)(2,1)S(1)}, u32[]{:S(2)}, u32[]{:S(2)}) %collective-permute-start.12) | collective-permute-done | bytes 163872 | tf_op jit(solution)/shard_map/ppermute | solution.py:282
  75.8 2.7 %collective-permute-done.13.rest_5_ = bf16[128,640]{1,0:T(8,128)(2,1)S(1)} collective-permute-done((bf16[128,640]{1,0:T(8,128)(2,1)S(1)}, bf16[128,640]{1,0:T(8,128)(2,1)S(1)}, u32[]{:S(2)}, u32[]{:S(2)}) %collective-permute-start.13) | collective-permute-done | bytes 163872 | tf_op jit(solution)/shard_map/ppermute | solution.py:282
  78.6 4.1 %shard_map.90 = (bf16[1024,1024]{1,0:T(8,128)(2,1)S(1)}, bf16[1024,640]{1,0:T(8,128)(2,1)S(1)}, bf16[128,384]{1,0:T(8,128)(2,1)S(1)}, bf16[128,384]{1,0:T(8,128)...) custom-call(s32[32]{0:T(128)S(1)} %copy-done.4, ...), custom_call_target="tpu_custom_call", output_to_operand_aliasing={{0}: (13, {})} | custom-call | flops 1845493760 | bytes 2097152 | tf_op jit(solution)/shard_map/pallas_call | solution.py:41
  82.7 2.2 %shard_map.92 = (bf16[128,384]{1,0:T(8,128)(2,1)S(1)}, bf16[128,384]{1,0:T(8,128)(2,1)S(1)}, bf16[128,384]{1,0:T(8,128)(2,1)S(1)}, bf16[128,384]{1,0:T(8,128)(2,...) custom-call(s32[32]{0:T(128)S(1)} %copy-done.4, ...), custom_call_target="tpu_custom_call" | custom-call | flops 838860800 | bytes 2097152 | tf_op jit(solution)/shard_map/pallas_call | solution.py:41
  85.6 7.2 %collective-permute-start.47 = (bf16[128,256]{1,0:T(8,128)(2,1)S(1)}, bf16[128,256]{1,0:T(8,128)(2,1)S(1)}, u32[]{:S(2)}, u32[]{:S(2)}) collective-permute-start(bf16[128,256]{1,0:T(8,128)(2,1)S(1)} %get-tuple-element.121), channel_id=1, source_target_pairs={{0,2},{1,3},{2,0},{3,1},{4,6},{5,7},{6,4},{7,5},{8,10},{9,11},{10,... | collective-permute-start | bytes 196616 | tf_op jit(solution)/shard_map/ppermute | solution.py:282
  95.9 2.5 %collective-permute-done.48.rest_3_ = bf16[128,256]{1,0:T(8,128)(2,1)S(1)} collective-permute-done((bf16[128,256]{1,0:T(8,128)(2,1)S(1)}, bf16[128,256]{1,0:T(8,128)(2,1)S(1)}, u32[]{:S(2)}, u32[]{:S(2)}) %collective-permute-start.48) | collective-permute-done | bytes 65568 | tf_op jit(solution)/shard_map/ppermute | solution.py:282
  100.0 2.3 %collective-permute-done.50.rest_5_ = bf16[128,256]{1,0:T(8,128)(2,1)S(1)} collective-permute-done((bf16[128,256]{1,0:T(8,128)(2,1)S(1)}, bf16[128,256]{1,0:T(8,128)(2,1)S(1)}, u32[]{:S(2)}, u32[]{:S(2)}) %collective-permute-start.50) | collective-permute-done | bytes 65568 | tf_op jit(solution)/shard_map/ppermute | solution.py:282
  104.9 3.4 %collective-permute-done.52.rest_7_ = bf16[128,256]{1,0:T(8,128)(2,1)S(1)} collective-permute-done((bf16[128,256]{1,0:T(8,128)(2,1)S(1)}, bf16[128,256]{1,0:T(8,128)(2,1)S(1)}, u32[]{:S(2)}, u32[]{:S(2)}) %collective-permute-start.52) | collective-permute-done | bytes 65568 | tf_op jit(solution)/shard_map/ppermute | solution.py:282
  108.3 2.3 %collective-permute-start.40 = (bf16[128,384]{1,0:T(8,128)(2,1)S(1)}, bf16[128,384]{1,0:T(8,128)(2,1)S(1)}, u32[]{:S(2)}, u32[]{:S(2)}) collective-permute-start(bf16[128,384]{1,0:T(8,128)(2,1)S(1)} %get-tuple-element.112), channel_id=1, source_target_pairs={{0,5},{1,4},{2,7},{3,6},{4,1},{5,0},{6,3},{7,2},{8,13},{9,12},{10,... | collective-permute-start | bytes 294920 | tf_op jit(solution)/shard_map/ppermute | solution.py:282
  112.6 1.9 %collective-permute-start.42 = (bf16[128,384]{1,0:T(8,128)(2,1)S(1)}, bf16[128,384]{1,0:T(8,128)(2,1)S(1)}, u32[]{:S(2)}, u32[]{:S(2)}) collective-permute-start(bf16[128,384]{1,0:T(8,128)(2,1)S(1)} %get-tuple-element.114), channel_id=1, source_target_pairs={{0,7},{1,6},{2,5},{3,4},{4,3},{5,2},{6,1},{7,0},{8,15},{9,14},{10,... | collective-permute-start | bytes 294920 | tf_op jit(solution)/shard_map/ppermute | solution.py:282
  114.5 7.4 %collective-permute-done.39.rest_4_ = bf16[128,384]{1,0:T(8,128)(2,1)S(1)} collective-permute-done((bf16[128,384]{1,0:T(8,128)(2,1)S(1)}, bf16[128,384]{1,0:T(8,128)(2,1)S(1)}, u32[]{:S(2)}, u32[]{:S(2)}) %collective-permute-start.39) | collective-permute-done | bytes 98336 | tf_op jit(solution)/shard_map/ppermute | solution.py:282
  124.5 2.7 %collective-permute-start.30 = (bf16[128,384]{1,0:T(8,128)(2,1)S(1)}, bf16[128,384]{1,0:T(8,128)(2,1)S(1)}, u32[]{:S(2)}, u32[]{:S(2)}) collective-permute-start(bf16[128,384]{1,0:T(8,128)(2,1)S(1)} %get-tuple-element.99), channel_id=1, source_target_pairs={{0,5},{1,4},{2,7},{3,6},{4,1},{5,0},{6,3},{7,2},{8,13},{9,12},{10,... | collective-permute-start | bytes 294920 | tf_op jit(solution)/shard_map/ppermute | solution.py:282
  131.6 2.3 %collective-permute-start.32 = (bf16[128,384]{1,0:T(8,128)(2,1)S(1)}, bf16[128,384]{1,0:T(8,128)(2,1)S(1)}, u32[]{:S(2)}, u32[]{:S(2)}) collective-permute-start(bf16[128,384]{1,0:T(8,128)(2,1)S(1)} %get-tuple-element.101), channel_id=1, source_target_pairs={{0,7},{1,6},{2,5},{3,4},{4,3},{5,2},{6,1},{7,0},{8,15},{9,14},{10,... | collective-permute-start | bytes 294920 | tf_op jit(solution)/shard_map/ppermute | solution.py:282
  135.0 3.7 %collective-permute-done.29.rest_4_ = bf16[128,384]{1,0:T(8,128)(2,1)S(1)} collective-permute-done((bf16[128,384]{1,0:T(8,128)(2,1)S(1)}, bf16[128,384]{1,0:T(8,128)(2,1)S(1)}, u32[]{:S(2)}, u32[]{:S(2)}) %collective-permute-start.29) | collective-permute-done | bytes 98336 | tf_op jit(solution)/shard_map/ppermute | solution.py:282
  140.6 2.5 %collective-permute-start.55 = (bf16[2,128,256]{2,1,0:T(8,128)(2,1)S(1)}, bf16[2,128,256]{2,1,0:T(8,128)(2,1)S(1)}, u32[]{:S(2)}, u32[]{:S(2)}) collective-permute-start(bf16[2,128,256]{2,1,0:T(8,128)(2,1)S(1)} %get-tuple-element.130), channel_id=1, source_target_pairs={{0,24},{8,16},{16,8},{24,0},{1,25},{9,17},{17,9},{25,1},{2,26},{10... | collective-permute-start | bytes 393224 | tf_op jit(solution)/shard_map/ppermute | solution.py:282
  143.6 5.4 %fusion = f32[1,1024,1024]{2,1,0:T(8,128)} fusion(f32[1,1024,1024]{2,1,0:T(8,128)S(1)} %copy-done.5, bf16[1024,1024]{1,0:T(8,128)(2,1)S(1)} %get-tuple-element.93, f32[]{:T(128)} %bitcast.1), kind=kOutput, calls=%fused_computation.1 | convolution fusion | flops 2150629376 | bytes 10485764 | tf_op jit(solution)/shard_map/dot_general | solution.py:345
  150.7 2.6 %collective-permute-start.45 = (bf16[2,128,384]{2,1,0:T(8,128)(2,1)S(1)}, bf16[2,128,384]{2,1,0:T(8,128)(2,1)S(1)}, u32[]{:S(2)}, u32[]{:S(2)}) collective-permute-start(bf16[2,128,384]{2,1,0:T(8,128)(2,1)S(1)} %get-tuple-element.118), channel_id=1, source_target_pairs={{0,24},{8,16},{16,8},{24,0},{1,25},{9,17},{17,9},{25,1},{2,26},{10... | collective-permute-start | bytes 589832 | tf_op jit(solution)/shard_map/ppermute | solution.py:282
  154.3 2.4 %collective-permute-start.35 = (bf16[2,128,384]{2,1,0:T(8,128)(2,1)S(1)}, bf16[2,128,384]{2,1,0:T(8,128)(2,1)S(1)}, u32[]{:S(2)}, u32[]{:S(2)}) collective-permute-start(bf16[2,128,384]{2,1,0:T(8,128)(2,1)S(1)} %get-tuple-element.105), channel_id=1, source_target_pairs={{0,24},{8,16},{16,8},{24,0},{1,25},{9,17},{17,9},{25,1},{2,26},{10... | collective-permute-start | bytes 589832 | tf_op jit(solution)/shard_map/ppermute | solution.py:282
  156.7 5.1 %fusion.1 = f32[1,1024,1024]{2,1,0:T(8,128)} fusion(f32[1,1024,1024]{2,1,0:T(8,128)S(1)} %copy-done.6, bf16[1024,1024]{1,0:T(8,128)(2,1)S(1)} %get-tuple-element.93, f32[]{:T(128)} %bitcast.1), kind=kOutput, calls=%fused_computation.3 | convolution fusion | flops 2150629376 | bytes 10485764 | tf_op jit(solution)/shard_map/dot_general | solution.py:343
  163.7 4.4 %collective-permute-done.34.rest_2_ = bf16[2,128,384]{2,1,0:T(8,128)(2,1)S(1)} collective-permute-done((bf16[2,128,384]{2,1,0:T(8,128)(2,1)S(1)}, bf16[2,128,384]{2,1,0:T(8,128)(2,1)S(1)}, u32[]{:S(2)}, u32[]{:S(2)}) %collective-permute-start.34) | collective-permute-done | bytes 196640 | tf_op jit(solution)/shard_map/ppermute | solution.py:282
  168.0 2.1 %shard_map.95 = bf16[128,8192]{1,0:T(8,128)(2,1)} custom-call(s32[32]{0:T(128)S(1)} %copy-done.4, bf16[2,128,384]{2,1,0:T(8,128)(2,1)S(1)} %get-tuple-element.102.rest_0_, bf16[2,128,384]{2,1,0:T(8,128)(2,1)S(1)} %collective-permute-done.33.rest_1_, bf16[2,128,384]{2,1,0:T(8,128)(2,1)S(1)} %collective-permute-done.34.rest_2_, ...), custom_call_target="tpu_custom_call" | custom-call | bytes 2097152 | tf_op jit(solution)/shard_map/pallas_call | solution.py:41
  (112 shorter events, 46.5 us)
Async XLA Ops:
  3.9 15.6 %collective-permute-start.16 = (bf16[2,128,384]{2,1,0:T(8,128)(2,1)S(1)}, bf16[2,128,384]{2,1,0:T(8,128)(2,1)S(1)}, u32[]{:S(2)}, u32[]{:S(2)}) collective-permute-start(bf16[2,128,384]{2,1,0:T(8,128)(2,1)S(1)} %get-tuple-element.80), channel_id=1, source_target_pairs={{0,8},{8,0},{16,24},{24,16},{1,9},{9,1},{17,25},{25,17},{2,10},{10... | collective-permute-start | bytes 589832 | tf_op jit(solution)/shard_map/ppermute | solution.py:282
  6.9 14.0 %collective-permute-start.17 = (bf16[2,128,384]{2,1,0:T(8,128)(2,1)S(1)}, bf16[2,128,384]{2,1,0:T(8,128)(2,1)S(1)}, u32[]{:S(2)}, u32[]{:S(2)}) collective-permute-start(bf16[2,128,384]{2,1,0:T(8,128)(2,1)S(1)} %get-tuple-element.81), channel_id=1, source_target_pairs={{0,16},{8,24},{16,0},{24,8},{1,17},{9,25},{17,1},{25,9},{2,18},{10... | collective-permute-start | bytes 589832 | tf_op jit(solution)/shard_map/ppermute | solution.py:282
  8.4 13.2 %collective-permute-start.18 = (bf16[2,128,384]{2,1,0:T(8,128)(2,1)S(1)}, bf16[2,128,384]{2,1,0:T(8,128)(2,1)S(1)}, u32[]{:S(2)}, u32[]{:S(2)}) collective-permute-start(bf16[2,128,384]{2,1,0:T(8,128)(2,1)S(1)} %get-tuple-element.82), channel_id=1, source_target_pairs={{0,24},{8,16},{16,8},{24,0},{1,25},{9,17},{17,9},{25,1},{2,26},{10... | collective-permute-start | bytes 589832 | tf_op jit(solution)/shard_map/ppermute | solution.py:282
  16.1 16.7 %collective-permute-start.6 = (bf16[2,128,640]{2,1,0:T(8,128)(2,1)S(1)}, bf16[2,128,640]{2,1,0:T(8,128)(2,1)S(1)}, u32[]{:S(2)}, u32[]{:S(2)}) collective-permute-start(bf16[2,128,640]{2,1,0:T(8,128)(2,1)S(1)} %get-tuple-element.68), channel_id=1, source_target_pairs={{0,8},{8,0},{16,24},{24,16},{1,9},{9,1},{17,25},{25,17},{2,10},{10... | collective-permute-start | bytes 983048 | tf_op jit(solution)/shard_map/ppermute | solution.py:282
  17.7 16.2 %collective-permute-start.7 = (bf16[2,128,640]{2,1,0:T(8,128)(2,1)S(1)}, bf16[2,128,640]{2,1,0:T(8,128)(2,1)S(1)}, u32[]{:S(2)}, u32[]{:S(2)}) collective-permute-start(bf16[2,128,640]{2,1,0:T(8,128)(2,1)S(1)} %get-tuple-element.69), channel_id=1, source_target_pairs={{0,16},{8,24},{16,0},{24,8},{1,17},{9,25},{17,1},{25,9},{2,18},{10... | collective-permute-start | bytes 983048 | tf_op jit(solution)/shard_map/ppermute | solution.py:282
  19.4 15.3 %collective-permute-start.8 = (bf16[2,128,640]{2,1,0:T(8,128)(2,1)S(1)}, bf16[2,128,640]{2,1,0:T(8,128)(2,1)S(1)}, u32[]{:S(2)}, u32[]{:S(2)}) collective-permute-start(bf16[2,128,640]{2,1,0:T(8,128)(2,1)S(1)} %get-tuple-element.70), channel_id=1, source_target_pairs={{0,24},{8,16},{16,8},{24,0},{1,25},{9,17},{17,9},{25,1},{2,26},{10... | collective-permute-start | bytes 983048 | tf_op jit(solution)/shard_map/ppermute | solution.py:282
  26.2 12.2 %collective-permute-start.19 = (bf16[128,384]{1,0:T(8,128)(2,1)S(1)}, bf16[128,384]{1,0:T(8,128)(2,1)S(1)}, u32[]{:S(2)}, u32[]{:S(2)}) collective-permute-start(bf16[128,384]{1,0:T(8,128)(2,1)S(1)} %get-tuple-element.84), channel_id=1, source_target_pairs={{0,1},{1,0},{2,3},{3,2},{4,5},{5,4},{6,7},{7,6},{8,9},{9,8},{10,11... | collective-permute-start | bytes 294920 | tf_op jit(solution)/shard_map/ppermute | solution.py:282
  38.3 18.9 %collective-permute-start.9 = (bf16[128,640]{1,0:T(8,128)(2,1)S(1)}, bf16[128,640]{1,0:T(8,128)(2,1)S(1)}, u32[]{:S(2)}, u32[]{:S(2)}) collective-permute-start(bf16[128,640]{1,0:T(8,128)(2,1)S(1)} %get-tuple-element.72), channel_id=1, source_target_pairs={{0,1},{1,0},{2,3},{3,2},{4,5},{5,4},{6,7},{7,6},{8,9},{9,8},{10,11... | collective-permute-start | bytes 491528 | tf_op jit(solution)/shard_map/ppermute | solution.py:282
  38.4 22.6 %collective-permute-start.10 = (bf16[128,640]{1,0:T(8,128)(2,1)S(1)}, bf16[128,640]{1,0:T(8,128)(2,1)S(1)}, u32[]{:S(2)}, u32[]{:S(2)}) collective-permute-start(bf16[128,640]{1,0:T(8,128)(2,1)S(1)} %get-tuple-element.73), channel_id=1, source_target_pairs={{0,2},{1,3},{2,0},{3,1},{4,6},{5,7},{6,4},{7,5},{8,10},{9,11},{10,... | collective-permute-start | bytes 491528 | tf_op jit(solution)/shard_map/ppermute | solution.py:282
  43.9 12.2 %collective-permute-start.25 = (bf16[128,384]{1,0:T(8,128)(2,1)S(1)}, bf16[128,384]{1,0:T(8,128)(2,1)S(1)}, u32[]{:S(2)}, u32[]{:S(2)}) collective-permute-start(bf16[128,384]{1,0:T(8,128)(2,1)S(1)} %get-tuple-element.90), channel_id=1, source_target_pairs={{0,7},{1,6},{2,5},{3,4},{4,3},{5,2},{6,1},{7,0},{8,15},{9,14},{10,... | collective-permute-start | bytes 294920 | tf_op jit(solution)/shard_map/ppermute | solution.py:282
  53.3 22.6 %collective-permute-start.12 = (bf16[128,640]{1,0:T(8,128)(2,1)S(1)}, bf16[128,640]{1,0:T(8,128)(2,1)S(1)}, u32[]{:S(2)}, u32[]{:S(2)}) collective-permute-start(bf16[128,640]{1,0:T(8,128)(2,1)S(1)} %get-tuple-element.75), channel_id=1, source_target_pairs={{0,4},{1,5},{2,6},{3,7},{4,0},{5,1},{6,2},{7,3},{8,12},{9,13},{10,... | collective-permute-start | bytes 491528 | tf_op jit(solution)/shard_map/ppermute | solution.py:282
  56.1 22.4 %collective-permute-start.13 = (bf16[128,640]{1,0:T(8,128)(2,1)S(1)}, bf16[128,640]{1,0:T(8,128)(2,1)S(1)}, u32[]{:S(2)}, u32[]{:S(2)}) collective-permute-start(bf16[128,640]{1,0:T(8,128)(2,1)S(1)} %get-tuple-element.76), channel_id=1, source_target_pairs={{0,5},{1,4},{2,7},{3,6},{4,1},{5,0},{6,3},{7,2},{8,13},{9,12},{10,... | collective-permute-start | bytes 491528 | tf_op jit(solution)/shard_map/ppermute | solution.py:282
  57.3 21.3 %collective-permute-start.14 = (bf16[128,640]{1,0:T(8,128)(2,1)S(1)}, bf16[128,640]{1,0:T(8,128)(2,1)S(1)}, u32[]{:S(2)}, u32[]{:S(2)}) collective-permute-start(bf16[128,640]{1,0:T(8,128)(2,1)S(1)} %get-tuple-element.77), channel_id=1, source_target_pairs={{0,6},{1,7},{2,4},{3,5},{4,2},{5,3},{6,0},{7,1},{8,14},{9,15},{10,... | collective-permute-start | bytes 491528 | tf_op jit(solution)/shard_map/ppermute | solution.py:282
  60.9 17.6 %collective-permute-start.15 = (bf16[128,640]{1,0:T(8,128)(2,1)S(1)}, bf16[128,640]{1,0:T(8,128)(2,1)S(1)}, u32[]{:S(2)}, u32[]{:S(2)}) collective-permute-start(bf16[128,640]{1,0:T(8,128)(2,1)S(1)} %get-tuple-element.78), channel_id=1, source_target_pairs={{0,7},{1,6},{2,5},{3,4},{4,3},{5,2},{6,1},{7,0},{8,15},{9,14},{10,... | collective-permute-start | bytes 491528 | tf_op jit(solution)/shard_map/ppermute | solution.py:282
  95.2 13.1 %collective-permute-start.26 = (bf16[128,384]{1,0:T(8,128)(2,1)S(1)}, bf16[128,384]{1,0:T(8,128)(2,1)S(1)}, u32[]{:S(2)}, u32[]{:S(2)}) collective-permute-start(bf16[128,384]{1,0:T(8,128)(2,1)S(1)} %get-tuple-element.95), channel_id=1, source_target_pairs={{0,1},{1,0},{2,3},{3,2},{4,5},{5,4},{6,7},{7,6},{8,9},{9,8},{10,11... | collective-permute-start | bytes 294920 | tf_op jit(solution)/shard_map/ppermute | solution.py:282
  95.8 14.8 %collective-permute-start.36 = (bf16[128,384]{1,0:T(8,128)(2,1)S(1)}, bf16[128,384]{1,0:T(8,128)(2,1)S(1)}, u32[]{:S(2)}, u32[]{:S(2)}) collective-permute-start(bf16[128,384]{1,0:T(8,128)(2,1)S(1)} %get-tuple-element.108), channel_id=1, source_target_pairs={{0,1},{1,0},{2,3},{3,2},{4,5},{5,4},{6,7},{7,6},{8,9},{9,8},{10,11... | collective-permute-start | bytes 294920 | tf_op jit(solution)/shard_map/ppermute | solution.py:282
  98.4 14.1 %collective-permute-start.37 = (bf16[128,384]{1,0:T(8,128)(2,1)S(1)}, bf16[128,384]{1,0:T(8,128)(2,1)S(1)}, u32[]{:S(2)}, u32[]{:S(2)}) collective-permute-start(bf16[128,384]{1,0:T(8,128)(2,1)S(1)} %get-tuple-element.109), channel_id=1, source_target_pairs={{0,2},{1,3},{2,0},{3,1},{4,6},{5,7},{6,4},{7,5},{8,10},{9,11},{10,... | collective-permute-start | bytes 294920 | tf_op jit(solution)/shard_map/ppermute | solution.py:282
  108.3 13.6 %collective-permute-start.39 = (bf16[128,384]{1,0:T(8,128)(2,1)S(1)}, bf16[128,384]{1,0:T(8,128)(2,1)S(1)}, u32[]{:S(2)}, u32[]{:S(2)}) collective-permute-start(bf16[128,384]{1,0:T(8,128)(2,1)S(1)} %get-tuple-element.111), channel_id=1, source_target_pairs={{0,4},{1,5},{2,6},{3,7},{4,0},{5,1},{6,2},{7,3},{8,12},{9,13},{10,... | collective-permute-start | bytes 294920 | tf_op jit(solution)/shard_map/ppermute | solution.py:282
  108.3 15.5 %collective-permute-start.40 = (bf16[128,384]{1,0:T(8,128)(2,1)S(1)}, bf16[128,384]{1,0:T(8,128)(2,1)S(1)}, u32[]{:S(2)}, u32[]{:S(2)}) collective-permute-start(bf16[128,384]{1,0:T(8,128)(2,1)S(1)} %get-tuple-element.112), channel_id=1, source_target_pairs={{0,5},{1,4},{2,7},{3,6},{4,1},{5,0},{6,3},{7,2},{8,13},{9,12},{10,... | collective-permute-start | bytes 294920 | tf_op jit(solution)/shard_map/ppermute | solution.py:282
  110.6 13.8 %collective-permute-start.41 = (bf16[128,384]{1,0:T(8,128)(2,1)S(1)}, bf16[128,384]{1,0:T(8,128)(2,1)S(1)}, u32[]{:S(2)}, u32[]{:S(2)}) collective-permute-start(bf16[128,384]{1,0:T(8,128)(2,1)S(1)} %get-tuple-element.113), channel_id=1, source_target_pairs={{0,6},{1,7},{2,4},{3,5},{4,2},{5,3},{6,0},{7,1},{8,14},{9,15},{10,... | collective-permute-start | bytes 294920 | tf_op jit(solution)/shard_map/ppermute | solution.py:282
  112.6 14.6 %collective-permute-start.42 = (bf16[128,384]{1,0:T(8,128)(2,1)S(1)}, bf16[128,384]{1,0:T(8,128)(2,1)S(1)}, u32[]{:S(2)}, u32[]{:S(2)}) collective-permute-start(bf16[128,384]{1,0:T(8,128)(2,1)S(1)} %get-tuple-element.114), channel_id=1, source_target_pairs={{0,7},{1,6},{2,5},{3,4},{4,3},{5,2},{6,1},{7,0},{8,15},{9,14},{10,... | collective-permute-start | bytes 294920 | tf_op jit(solution)/shard_map/ppermute | solution.py:282
  114.5 17.1 %collective-permute-start.27 = (bf16[128,384]{1,0:T(8,128)(2,1)S(1)}, bf16[128,384]{1,0:T(8,128)(2,1)S(1)}, u32[]{:S(2)}, u32[]{:S(2)}) collective-permute-start(bf16[128,384]{1,0:T(8,128)(2,1)S(1)} %get-tuple-element.96), channel_id=1, source_target_pairs={{0,2},{1,3},{2,0},{3,1},{4,6},{5,7},{6,4},{7,5},{8,10},{9,11},{10,... | collective-permute-start | bytes 294920 | tf_op jit(solution)/shard_map/ppermute | solution.py:282
  123.8 14.9 %collective-permute-start.29 = (bf16[128,384]{1,0:T(8,128)(2,1)S(1)}, bf16[128,384]{1,0:T(8,128)(2,1)S(1)}, u32[]{:S(2)}, u32[]{:S(2)}) collective-permute-start(bf16[128,384]{1,0:T(8,128)(2,1)S(1)} %get-tuple-element.98), channel_id=1, source_target_pairs={{0,4},{1,5},{2,6},{3,7},{4,0},{5,1},{6,2},{7,3},{8,12},{9,13},{10,... | collective-permute-start | bytes 294920 | tf_op jit(solution)/shard_map/ppermute | solution.py:282
  124.5 16.1 %collective-permute-start.30 = (bf16[128,384]{1,0:T(8,128)(2,1)S(1)}, bf16[128,384]{1,0:T(8,128)(2,1)S(1)}, u32[]{:S(2)}, u32[]{:S(2)}) collective-permute-start(bf16[128,384]{1,0:T(8,128)(2,1)S(1)} %get-tuple-element.99), channel_id=1, source_target_pairs={{0,5},{1,4},{2,7},{3,6},{4,1},{5,0},{6,3},{7,2},{8,13},{9,12},{10,... | collective-permute-start | bytes 294920 | tf_op jit(solution)/shard_map/ppermute | solution.py:282
  127.2 15.9 %collective-permute-start.31 = (bf16[128,384]{1,0:T(8,128)(2,1)S(1)}, bf16[128,384]{1,0:T(8,128)(2,1)S(1)}, u32[]{:S(2)}, u32[]{:S(2)}) collective-permute-start(bf16[128,384]{1,0:T(8,128)(2,1)S(1)} %get-tuple-element.100), channel_id=1, source_target_pairs={{0,6},{1,7},{2,4},{3,5},{4,2},{5,3},{6,0},{7,1},{8,14},{9,15},{10,... | collective-permute-start | bytes 294920 | tf_op jit(solution)/shard_map/ppermute | solution.py:282
  131.6 17.5 %collective-permute-start.32 = (bf16[128,384]{1,0:T(8,128)(2,1)S(1)}, bf16[128,384]{1,0:T(8,128)(2,1)S(1)}, u32[]{:S(2)}, u32[]{:S(2)}) collective-permute-start(bf16[128,384]{1,0:T(8,128)(2,1)S(1)} %get-tuple-element.101), channel_id=1, source_target_pairs={{0,7},{1,6},{2,5},{3,4},{4,3},{5,2},{6,1},{7,0},{8,15},{9,14},{10,... | collective-permute-start | bytes 294920 | tf_op jit(solution)/shard_map/ppermute | solution.py:282
  133.9 16.8 %collective-permute-start.53 = (bf16[2,128,256]{2,1,0:T(8,128)(2,1)S(1)}, bf16[2,128,256]{2,1,0:T(8,128)(2,1)S(1)}, u32[]{:S(2)}, u32[]{:S(2)}) collective-permute-start(bf16[2,128,256]{2,1,0:T(8,128)(2,1)S(1)} %get-tuple-element.128), channel_id=1, source_target_pairs={{0,8},{8,0},{16,24},{24,16},{1,9},{9,1},{17,25},{25,17},{2,10},{10... | collective-permute-start | bytes 393224 | tf_op jit(solution)/shard_map/ppermute | solution.py:282
  138.7 14.6 %collective-permute-start.54 = (bf16[2,128,256]{2,1,0:T(8,128)(2,1)S(1)}, bf16[2,128,256]{2,1,0:T(8,128)(2,1)S(1)}, u32[]{:S(2)}, u32[]{:S(2)}) collective-permute-start(bf16[2,128,256]{2,1,0:T(8,128)(2,1)S(1)} %get-tuple-element.129), channel_id=1, source_target_pairs={{0,16},{8,24},{16,0},{24,8},{1,17},{9,25},{17,1},{25,9},{2,18},{10... | collective-permute-start | bytes 393224 | tf_op jit(solution)/shard_map/ppermute | solution.py:282
  140.6 13.1 %collective-permute-start.55 = (bf16[2,128,256]{2,1,0:T(8,128)(2,1)S(1)}, bf16[2,128,256]{2,1,0:T(8,128)(2,1)S(1)}, u32[]{:S(2)}, u32[]{:S(2)}) collective-permute-start(bf16[2,128,256]{2,1,0:T(8,128)(2,1)S(1)} %get-tuple-element.130), channel_id=1, source_target_pairs={{0,24},{8,16},{16,8},{24,0},{1,25},{9,17},{17,9},{25,1},{2,26},{10... | collective-permute-start | bytes 393224 | tf_op jit(solution)/shard_map/ppermute | solution.py:282
  149.0 12.8 %collective-permute-start.44 = (bf16[2,128,384]{2,1,0:T(8,128)(2,1)S(1)}, bf16[2,128,384]{2,1,0:T(8,128)(2,1)S(1)}, u32[]{:S(2)}, u32[]{:S(2)}) collective-permute-start(bf16[2,128,384]{2,1,0:T(8,128)(2,1)S(1)} %get-tuple-element.117), channel_id=1, source_target_pairs={{0,16},{8,24},{16,0},{24,8},{1,17},{9,25},{17,1},{25,9},{2,18},{10... | collective-permute-start | bytes 589832 | tf_op jit(solution)/shard_map/ppermute | solution.py:282
  153.7 14.3 %collective-permute-start.34 = (bf16[2,128,384]{2,1,0:T(8,128)(2,1)S(1)}, bf16[2,128,384]{2,1,0:T(8,128)(2,1)S(1)}, u32[]{:S(2)}, u32[]{:S(2)}) collective-permute-start(bf16[2,128,384]{2,1,0:T(8,128)(2,1)S(1)} %get-tuple-element.104), channel_id=1, source_target_pairs={{0,16},{8,24},{16,0},{24,8},{1,17},{9,25},{17,1},{25,9},{2,18},{10... | collective-permute-start | bytes 589832 | tf_op jit(solution)/shard_map/ppermute | solution.py:282
  154.3 13.8 %collective-permute-start.35 = (bf16[2,128,384]{2,1,0:T(8,128)(2,1)S(1)}, bf16[2,128,384]{2,1,0:T(8,128)(2,1)S(1)}, u32[]{:S(2)}, u32[]{:S(2)}) collective-permute-start(bf16[2,128,384]{2,1,0:T(8,128)(2,1)S(1)} %get-tuple-element.105), channel_id=1, source_target_pairs={{0,24},{8,16},{16,8},{24,0},{1,25},{9,17},{17,9},{25,1},{2,26},{10... | collective-permute-start | bytes 589832 | tf_op jit(solution)/shard_map/ppermute | solution.py:282
  (31 other events, 407.2 us)

commit v2 on v1

v2 whole, which is shorter than its diff:
```python
import jax
import jax.numpy as jnp
from jax import lax
from jax.experimental import pallas as pl
from jax.experimental.pallas import tpu as pltpu
from jax.sharding import PartitionSpec as P


clip_level = 0.5
beta_stat = 0.95

FORWARD = (2, 4, 2)
BACKWARD = (4, 2, 2)
ANY = pl.BlockSpec(memory_space=pl.ANY)
SMEM = pl.BlockSpec(memory_space=pltpu.SMEM)
VMEM = pl.BlockSpec(memory_space=pltpu.VMEM)
HBM = pl.BlockSpec(memory_space=pltpu.HBM)


def spans(parts, size):
    total, at, out = sum(parts), 0, []
    for part in parts:
        out.append((at * size // total, part * size // total))
        at += part
    return out


def high(value, count):
    return value >> (count.bit_length() - 1) if count & (count - 1) == 0 else value // count


def low(value, count):
    return value & (count - 1) if count & (count - 1) == 0 else value % count


def column_slots(owner, me, mp, group):
    distances = [high(owner[me * mp + c], mp) ^ me for c in range(mp)]
    return [
        k * group + sum([(other == k).astype(jnp.int32) for other in distances[:c]], jnp.int32(0))
        for c, k in enumerate(distances)
    ]


def list_slots(owner, slots, me, dp, mp, group):
    owners = [owner[b] for b in range(dp * mp)]
    found = []
    for band in range(dp):
        last = [jnp.int32(0)] * group
        for o in owners[band * mp : (band + 1) * mp]:
            match = high(o, mp) == me
            last = [jnp.where(match, new, old) for new, old in zip(last[1:] + [low(o, mp)], last)]
        found.append(last)
    for band in range(dp):
        for rank, m in enumerate(found[band]):
            slots[m] = (band ^ me) * group + rank


def call(body, outs, inputs, table, scratch=(), ins=VMEM, out=VMEM, aliases=None, flops=0, mib=8):
    ins = ins if isinstance(ins, list) else [ins] * len(inputs)
    out = out if isinstance(out, list) else [out] * len(outs)
    return pl.pallas_call(
        body,
        out_shape=outs,
        in_specs=[SMEM] + ins,
        out_specs=out,
        scratch_shapes=list(scratch),
        input_output_aliases=aliases or {},
        cost_estimate=pl.CostEstimate(flops=flops, bytes_accessed=1 << 21, transcendentals=0),
        compiler_params=pltpu.CompilerParams(vmem_limit_bytes=mib << 20),
    )(table, *inputs)


def pack_first(grad, owner, dp, mp, blk, cut):
    rows = grad.shape[0]
    group = mp // dp
    at, width = cut

    def body(grad, owner_ref, *rest):
        outs, (plan, owner, buf, sems) = rest[:dp], rest[dp:]
        table = pltpu.make_async_copy(owner_ref, owner, sems.at[mp])
        table.start()
        copies = [
            pltpu.make_async_copy(grad.at[:, pl.ds(c * blk + at, width)], buf.at[c], sems.at[c])
            for c in range(mp)
        ]
        for copy in copies:
            copy.start()
        table.wait()
        slots = column_slots(owner, lax.axis_index("dp"), mp, group)
        for c, slot in enumerate(slots):
            plan[slot] = c
        for c, slot in enumerate(slots):
            copies[c].wait()
            for k in range(dp):

                @pl.when(high(slot, group) == k)
                def _(k=k, c=c, slot=slot):
                    outs[k][low(slot, group)] = buf[c]

    outs = [jax.ShapeDtypeStruct((group, rows, width), grad.dtype)] * dp
    outs.append(jax.ShapeDtypeStruct((mp,), jnp.int32))
    flat = pl.pallas_call(
        body,
        out_shape=outs,
        in_specs=[HBM, HBM],
        out_specs=[VMEM] * dp + [SMEM],
        scratch_shapes=[
            pltpu.SMEM(owner.shape, jnp.int32),
            pltpu.VMEM((mp, rows, width), grad.dtype),
            pltpu.SemaphoreType.DMA((mp + 1,)),
        ],
        cost_estimate=pl.CostEstimate(flops=0, bytes_accessed=1 << 21, transcendentals=0),
        compiler_params=pltpu.CompilerParams(vmem_limit_bytes=8 << 20),
        name="pack0",
    )(
        pltpu.with_memory_space_constraint(grad, pltpu.HBM),
        pltpu.with_memory_space_constraint(owner, pltpu.HBM),
    )
    return flat[:dp], flat[dp]


def pack(grad, plan, owner, dp, mp, blk, cut):
    rows = grad.shape[0]
    group = mp // dp
    at, width = cut

    def body(plan, grad, *rest):
        rest = list(rest)
        owner_ref = None if owner is None else rest.pop(0)
        outs, sems = rest[:dp], rest[-1]
        copies = []
        for k in list(range(1, dp)) + [0]:
            for j in range(group):
                start = pl.multiple_of(plan[k * group + j] * blk + at, 128)
                copy = pltpu.make_async_copy(
                    grad.at[:, pl.ds(start, width)], outs[k].at[j], sems.at[k * group + j]
                )
                copy.start()
                copies.append(copy)
        if owner is not None:
            list_slots(owner_ref, rest[dp], lax.axis_index("dp"), dp, mp, group)
        for copy in copies:
            copy.wait()

    outs = [jax.ShapeDtypeStruct((group, rows, width), grad.dtype)] * dp
    out, inputs, ins = [VMEM] * dp, [pltpu.with_memory_space_constraint(grad, pltpu.HBM)], [HBM]
    if owner is not None:
        outs.append(jax.ShapeDtypeStruct((mp,), jnp.int32))
        out, inputs, ins = out + [SMEM], inputs + [owner], ins + [SMEM]
    flat = call(body, outs, inputs, plan, [pltpu.SemaphoreType.DMA((mp,))], ins=ins, out=out)
    return flat[:dp], flat[dp:]


def square_sum(grad, plan):
    rows, cols = grad.shape
    step = min(1024, cols)

    def body(plan, grad, out):
        total = jnp.zeros((8, step), jnp.float32)
        for i in range(cols // step):
            values = grad[:, i * step : (i + 1) * step].astype(jnp.float32)
            total = total + jnp.sum((values * values).reshape(rows // 8, 8, step), axis=0)
        out[...] = jnp.full(out.shape, jnp.sum(total), jnp.float32)

    return call(body, [jax.ShapeDtypeStruct((8, 128), jnp.float32)], [grad], plan)[0]


def route(got, plan, dp, mp):
    group, rows, width = got[0].shape

    def body(plan, *rest):
        got, outs = rest[:dp], rest[dp:]
        mine = lax.axis_index("mp")
        for kk in range(mp):
            entry = plan[mine ^ kk]
            for k in range(dp):

                @pl.when(high(entry, group) == k)
                def _(k=k, kk=kk, entry=entry):
                    outs[kk][...] = got[k][low(entry, group)]

    outs = [jax.ShapeDtypeStruct((rows, width), got[0].dtype)] * mp
    return call(body, outs, got, plan)


def unroute(pieces, plan, dp, mp):
    rows, width = pieces[0].shape
    group = mp // dp

    def body(plan, *rest):
        pieces, outs = rest[:mp], rest[mp:]
        mine = lax.axis_index("mp")
        for kk in range(mp):
            entry = plan[mine ^ kk]
            for k in range(dp):

                @pl.when(high(entry, group) == k)
                def _(k=k, kk=kk, entry=entry):
                    outs[k][low(entry, group)] = pieces[kk][...]

    outs = [jax.ShapeDtypeStruct((group, rows, width), pieces[0].dtype)] * dp
    return call(body, outs, list(pieces), plan)


def place(parts, old, plan, dp, mp, blk, cuts):
    group, rows = parts[0][0].shape[:2]
    count = len(cuts)

    def body(plan, *rest):
        parts, out, sems = rest[: count * dp], rest[-2], rest[-1]
        copies = []
        for k in range(dp):
            for j in range(group):
                for c, (at, width) in enumerate(cuts):
                    start = pl.multiple_of(plan[k * group + j] * blk + at, 128)
                    copy = pltpu.make_async_copy(
                        parts[c * dp + k].at[j],
                        out.at[:, pl.ds(start, width)],
                        sems.at[(c * dp + k) * group + j],
                    )
                    copy.start()
                    copies.append(copy)
        for copy in copies:
            copy.wait()

    outs = [jax.ShapeDtypeStruct((rows, mp * blk), parts[0][0].dtype)]
    inputs = [part for chunk in parts for part in chunk]
    ins = [VMEM] * len(inputs)
    aliases = None
    if old is not None:
        aliases = {1 + len(inputs): 0}
        inputs, ins = inputs + [old], ins + [ANY]
    scratch = [pltpu.SemaphoreType.DMA((mp * count,))]
    return call(body, outs, inputs, plan, scratch, ins, ANY, aliases)[0]


def gather(pieces, block, mp, at, width):
    rows = pieces[0].shape[0]
    mine = lax.axis_index("mp")
    for kk in range(mp):
        start = pl.multiple_of((mine ^ kk) * rows, 16)
        block[pl.ds(start, rows), at : at + width] = pieces[kk][...]


def partial_update(pieces, left_root, right_root, old, plan, mp, at, width):
    blk = left_root.shape[0]
    tile = min(512, blk)

    def body(plan, *rest):
        pieces = rest[:mp]
        left, right = rest[mp : mp + 2]
        block, total = rest[-2:]
        gather(pieces, block, mp, at, width)

        @pl.loop(0, blk // tile)
        def _(i):
            span = pl.ds(pl.multiple_of(i * tile, tile), tile)
            half = jnp.dot(left[span, :], block[:, at : at + width], preferred_element_type=jnp.float32)
            term = jnp.dot(
                half.astype(block.dtype), right[at : at + width, :], preferred_element_type=jnp.float32
            )
            total[span, :] = term if old is None else total[span, :] + term

    outs = [
        jax.ShapeDtypeStruct((blk, blk), pieces[0].dtype),
        jax.ShapeDtypeStruct((blk, blk), jnp.float32),
    ]
    inputs = [*pieces, left_root, right_root, *(old or ())]
    aliases = None if old is None else {mp + 3: 0, mp + 4: 1}
    return call(body, outs, inputs, plan, aliases=aliases, flops=4 * blk * blk * width, mib=24)


def deal(update, outs, rows, mp, cuts):
    mine = lax.axis_index("mp")
    for c, (start, size) in enumerate(cuts):
        for kk in range(mp):
            row = pl.multiple_of((mine ^ kk) * rows, 16)
            outs[c * mp + kk][...] = update[pl.ds(row, rows), start : start + size]


def last_update(pieces, left_root, right_root, block, total, scale, plan, mp, at, width, cut):
    rows = pieces[0].shape[0]
    blk = left_root.shape[0]
    tile = min(512, blk)
    start, size = cut

    def body(plan, *rest):
        pieces = rest[:mp]
        left, right, total, scale, _, block, half = rest[mp : mp + 7]
        outs, update = rest[mp + 7 : -1], rest[-1]
        gather(pieces, block, mp, at, width)
        scaling = scale[0:1, 0:1]

        @pl.loop(0, blk // tile)
        def _(i):
            span = pl.ds(pl.multiple_of(i * tile, tile), tile)
            term = jnp.dot(left[span, :], block[:, at : at + width], preferred_element_type=jnp.float32)
            half[span, :] = term.astype(half.dtype)
            term = jnp.dot(
                term.astype(half.dtype),
                right[at : at + width, start : start + size],
                preferred_element_type=jnp.float32,
            )
            update[span, :] = ((total[span, start : start + size] + term) * scaling).astype(update.dtype)

        deal(update, outs, rows, mp, [(0, size)])

    dtype = pieces[0].dtype
    outs = [jax.ShapeDtypeStruct((blk, blk), dtype), jax.ShapeDtypeStruct((blk, width), dtype)]
    outs += [jax.ShapeDtypeStruct((rows, size), dtype)] * mp
    scratch = [pltpu.VMEM((blk, size), dtype)]
    inputs = [*pieces, left_root, right_root, total, scale, block]
    flops = 2 * blk * width * (blk + size)
    flat = call(body, outs, inputs, plan, scratch, aliases={mp + 5: 0}, flops=flops, mib=24)
    return flat[0], flat[1], flat[2:]


def rest_update(half, right_root, total, scale, rows, plan, mp, at, cuts):
    blk, width = half.shape
    tile = min(512, blk)
    base = cuts[0][0]

    def body(plan, half, right, total, scale, *rest):
        outs, update = rest[:-1], rest[-1]
        scaling = scale[0:1, 0:1]

        @pl.loop(0, blk // tile)
        def _(i):
            span = pl.ds(pl.multiple_of(i * tile, tile), tile)
            term = jnp.dot(half[span, :], right[at : at + width, base:], preferred_element_type=jnp.float32)
            update[span, :] = ((total[span, base:] + term) * scaling).astype(update.dtype)

        deal(update, outs, rows, mp, [(start - base, size) for start, size in cuts])

    outs = [jax.ShapeDtypeStruct((rows, size), half.dtype) for _, size in cuts for _ in range(mp)]
    scratch = [pltpu.VMEM((blk, blk - base), half.dtype)]
    flops = 2 * blk * width * (blk - base)
    flat = call(body, outs, [half, right_root, total, scale], plan, scratch, flops=flops, mib=24)
    return [flat[c * mp : (c + 1) * mp] for c in range(len(cuts))]


def swap(value, axis, distance):
    count = lax.axis_size(axis)
    return lax.ppermute(value, axis, [(i, i ^ distance) for i in range(count)])


def per_device(grad, owner, left_stat, right_stat, left_root, right_root):
    dp, mp = lax.axis_size("dp"), lax.axis_size("mp")
    blk = left_root.shape[-1]
    left_root, right_root = left_root[0], right_root[0]
    forward, backward = spans(FORWARD, blk), spans(BACKWARD, blk)

    chunk, plan = pack_first(grad, owner, dp, mp, blk, forward[0])
    packed, slots = [chunk], None
    for c, cut in enumerate(forward[1:], 1):
        chunk, found = pack(grad, plan, owner if slots is None else None, dp, mp, blk, cut)
        packed.append(chunk)
        slots = found[0] if found else slots
    crossed = [[part if k == 0 else swap(part, "dp", k) for k, part in enumerate(chunk)] for chunk in packed]
    total = square_sum(grad, plan)
    total = total + swap(total, "mp", 1)
    terms = [swap(total, "mp", k) for k in range(2, mp, 2)]
    total = sum(terms, total)
    terms = [swap(total, "dp", k) for k in range(1, dp)]
    total = sum(terms, total)
    mean_square = total / (grad.size * dp * mp)
    scale = clip_level / jnp.sqrt(mean_square + 1e-06)
    factor = (1.0 - beta_stat) * scale * scale / blk

    arrived = []
    for c in range(len(forward)):
        pieces = route(crossed[c], slots, dp, mp)
        moved = list(pieces)
        for k in range(1, mp):
            moved[k] = swap(pieces[k], "mp", k)
        arrived.append(moved)

    state = None
    for c, (at, width) in enumerate(forward[:-1]):
        state = partial_update(arrived[c], left_root, right_root, state, plan, mp, at, width)
    at, width = forward[-1]
    rows = arrived[0][0].shape[0]
    block, half, first = last_update(
        arrived[-1], left_root, right_root, *state, scale, plan, mp, at, width, backward[0]
    )
    leaving = [first] + rest_update(half, right_root, state[1], scale, rows, plan, mp, at, backward[1:])

    parts = []
    for c in range(len(backward)):
        pieces = list(leaving[c])
        for k in range(1, mp):
            pieces[k] = swap(leaving[c][k], "mp", k)
        chunk = list(unroute(pieces, slots, dp, mp))
        for k in range(1, dp):
            chunk[k] = swap(chunk[k], "dp", k)
        parts.append(chunk)
    out = place(parts[:-1], None, plan, dp, mp, blk, backward[:-1])
    out = place(parts[-1:], out, plan, dp, mp, blk, backward[-1:])

    factor = factor[0, 0]
    left_gram = jnp.dot(block, block.T, preferred_element_type=jnp.float32)
    left_new = beta_stat * left_stat[0] + factor * left_gram
    right_gram = jnp.dot(block.T, block, preferred_element_type=jnp.float32)
    right_new = beta_stat * right_stat[0] + factor * right_gram
    return (left_new[None], right_new[None], out)


def solution(mesh):
    split = P(("dp", "mp"), None, None)
    rows = P(("dp", "mp"), None)

    return jax.shard_map(
        per_device,
        mesh=mesh,
        in_specs=(rows, P(), split, split, split, split),
        out_specs=(split, split, rows),
        check_vma=False,
    )
```

time: 171 us -> 188 us (1.099)
  waiting for transfers between devices: 60.3 us -> 69.8 us
  starting transfers between devices: 75 us -> 79.4 us
  Pallas kernels: 20.5 us -> 24.6 us
    ppermute x56 -> x67, waiting for transfers between devices: 60.3 us -> 69.8 us  [swap(): return lax.ppermute(value, axis, [(i, i ^ distance) for i in range(count)])]
    ppermute x56 -> x67, starting transfers between devices: 75 us -> 79.4 us  [swap(): return lax.ppermute(value, axis, [(i, i ^ distance) for i in range(count)])]
    pallas_call x11 -> x16, Pallas kernels: 20.5 us -> 24.6 us  [the longest x15 22.8 us: call(): pl.pallas_call(body, out_shape=outs, in_specs=[SMEM] + ins, out_specs=out...]
  transfers between devices with their start and end apart: 56 -> 67, of which waited for: 19 -> 19; matrix products, arithmetic and copies ran while one was open for 6% -> 6% of each run, Pallas kernels for 6% -> 9%
where the time goes in v2:
time: 188 us; the launch traced here: 187 us
  starting transfers between devices  79.4 us (42%)
  waiting for transfers between devices  69.8 us (37%)
  Pallas kernels  24.6 us (13%)
  matrix products  10.5 us (6%)
  local copies, waits for them, and re-layouts  2.12 us (1%)
    ppermute x67, starting transfers between devices, swap(): return lax.ppermute(value, axis, [(i, i ^ distance) for i in range(count)])  79.4 us
    ppermute x67, waiting for transfers between devices, swap(): return lax.ppermute(value, axis, [(i, i ^ distance) for i in range(count)])  69.8 us
    pallas_call x15, Pallas kernels, call(): pl.pallas_call(body, out_shape=outs, in_specs=[SMEM] + ins, out_specs=out...  22.8 us
    dot_general x1, matrix products, per_device(): right_gram = jnp.dot(block.T, block, preferred_element_type=jnp.float32)  5.37 us
    dot_general x1, matrix products, per_device(): left_gram = jnp.dot(block, block.T, preferred_element_type=jnp.float32)  5.08 us
  transfers between devices with their start and end apart: 67, of which 19 were waited for; matrix products, arithmetic and copies ran while one was open for 6% of the time, Pallas kernels for 9%

profile of v2, /device:TPU:0, one launch (start us, length us, event | category | flops | bytes accessed | tf_op | source)
XLA Modules:
  0.0 187.5 jit_solution(17895403774958082096)
XLA Ops:
  6.2 2.9 %collective-permute-start.1 = (f32[8,128]{1,0:T(8,128)S(1)}, f32[8,128]{1,0:T(8,128)S(1)}, u32[]{:S(2)}, u32[]{:S(2)}) collective-permute-start(f32[8,128]{1,0:T(8,128)S(1)} %add.33), channel_id=1, source_target_pairs={{0,2},{1,3},{2,0},{3,1},{4,6},{5,7},{6,4},{7,5},{8,10},{9,11},{10,... | collective-permute-start | bytes 12296 | tf_op jit(solution)/shard_map/ppermute | solution.py:344
  9.1 2.6 %collective-permute-start.2 = (f32[8,128]{1,0:T(8,128)S(1)}, f32[8,128]{1,0:T(8,128)S(1)}, u32[]{:S(2)}, u32[]{:S(2)}) collective-permute-start(f32[8,128]{1,0:T(8,128)S(1)} %add.33), channel_id=1, source_target_pairs={{0,4},{1,5},{2,6},{3,7},{4,0},{5,1},{6,2},{7,3},{8,12},{9,13},{10,... | collective-permute-start | bytes 12296 | tf_op jit(solution)/shard_map/ppermute | solution.py:344
  19.0 4.8 %collective-permute-done.4 = f32[8,128]{1,0:T(8,128)S(1)} collective-permute-done((f32[8,128]{1,0:T(8,128)S(1)}, f32[8,128]{1,0:T(8,128)S(1)}, u32[]{:S(2)}, u32[]{:S(2)}) %collective-permute-start.4) | collective-permute-done | bytes 4128 | tf_op jit(solution)/shard_map/ppermute | solution.py:344
  25.2 2.1 %collective-permute-done.5 = f32[8,128]{1,0:T(8,128)S(1)} collective-permute-done((f32[8,128]{1,0:T(8,128)S(1)}, f32[8,128]{1,0:T(8,128)S(1)}, u32[]{:S(2)}, u32[]{:S(2)}) %collective-permute-start.5) | collective-permute-done | bytes 4128 | tf_op jit(solution)/shard_map/ppermute | solution.py:344
  28.8 2.5 %shard_map.86 = (bf16[2,128,512]{2,1,0:T(8,128)(2,1)S(1)}, bf16[2,128,512]{2,1,0:T(8,128)(2,1)S(1)}, bf16[2,128,512]{2,1,0:T(8,128)(2,1)S(1)}, bf16[2,128,512]{2,1,0:T(8,128)(2,1)S(1)}, s32[8]{0:T(128)S(1)}) custom-call(s32[8]{0:T(128)S(1)} %get-tuple-element.83.plan, bf16[128,8192]{1,0:T(8,128)(2,1)} %grad.7, s32[32]{0:T(128)S(1)} %copy-done.3), custom_call_target="tpu_custom_call" | custom-call | bytes 2097152 | tf_op jit(solution)/shard_map/pallas_call | solution.py:61
  38.6 10.0 %collective-permute-done.8.rest_2_ = bf16[2,128,256]{2,1,0:T(8,128)(2,1)S(1)} collective-permute-done((bf16[2,128,256]{2,1,0:T(8,128)(2,1)S(1)}, bf16[2,128,256]{2,1,0:T(8,128)(2,1)S(1)}, u32[]{:S(2)}, u32[]{:S(2)}) %collective-permute-start.8) | collective-permute-done | bytes 131104 | tf_op jit(solution)/shard_map/ppermute | solution.py:344
  50.5 3.2 %collective-permute-start.33 = (bf16[128,256]{1,0:T(8,128)(2,1)S(1)}, bf16[128,256]{1,0:T(8,128)(2,1)S(1)}, u32[]{:S(2)}, u32[]{:S(2)}) collective-permute-start(bf16[128,256]{1,0:T(8,128)(2,1)S(1)} %get-tuple-element.117), channel_id=1, source_target_pairs={{0,4},{1,5},{2,6},{3,7},{4,0},{5,1},{6,2},{7,3},{8,12},{9,13},{10,... | collective-permute-start | bytes 196616 | tf_op jit(solution)/shard_map/ppermute | solution.py:344
  53.8 2.8 %collective-permute-start.35 = (bf16[128,256]{1,0:T(8,128)(2,1)S(1)}, bf16[128,256]{1,0:T(8,128)(2,1)S(1)}, u32[]{:S(2)}, u32[]{:S(2)}) collective-permute-start(bf16[128,256]{1,0:T(8,128)(2,1)S(1)} %get-tuple-element.119), channel_id=1, source_target_pairs={{0,6},{1,7},{2,4},{3,5},{4,2},{5,3},{6,0},{7,1},{8,14},{9,15},{10,... | collective-permute-start | bytes 196616 | tf_op jit(solution)/shard_map/ppermute | solution.py:344
  59.5 2.8 %collective-permute-done.34.rest_5_ = bf16[128,256]{1,0:T(8,128)(2,1)S(1)} collective-permute-done((bf16[128,256]{1,0:T(8,128)(2,1)S(1)}, bf16[128,256]{1,0:T(8,128)(2,1)S(1)}, u32[]{:S(2)}, u32[]{:S(2)}) %collective-permute-start.34) | collective-permute-done | bytes 65568 | tf_op jit(solution)/shard_map/ppermute | solution.py:344
  62.2 2.1 %collective-permute-start.10 = (bf16[128,256]{1,0:T(8,128)(2,1)S(1)}, bf16[128,256]{1,0:T(8,128)(2,1)S(1)}, u32[]{:S(2)}, u32[]{:S(2)}) collective-permute-start(bf16[128,256]{1,0:T(8,128)(2,1)S(1)} %get-tuple-element.90), channel_id=1, source_target_pairs={{0,1},{1,0},{2,3},{3,2},{4,5},{5,4},{6,7},{7,6},{8,9},{9,8},{10,11... | collective-permute-start | bytes 196616 | tf_op jit(solution)/shard_map/ppermute | solution.py:344
  66.8 2.4 %collective-permute-done.11.rest_2_ = bf16[128,256]{1,0:T(8,128)(2,1)S(1)} collective-permute-done((bf16[128,256]{1,0:T(8,128)(2,1)S(1)}, bf16[128,256]{1,0:T(8,128)(2,1)S(1)}, u32[]{:S(2)}, u32[]{:S(2)}) %collective-permute-start.11) | collective-permute-done | bytes 65568 | tf_op jit(solution)/shard_map/ppermute | solution.py:344
  70.8 4.1 %collective-permute-start.26 = (bf16[128,512]{1,0:T(8,128)(2,1)S(1)}, bf16[128,512]{1,0:T(8,128)(2,1)S(1)}, u32[]{:S(2)}, u32[]{:S(2)}) collective-permute-start(bf16[128,512]{1,0:T(8,128)(2,1)S(1)} %get-tuple-element.108), channel_id=1, source_target_pairs={{0,7},{1,6},{2,5},{3,4},{4,3},{5,2},{6,1},{7,0},{8,15},{9,14},{10,... | collective-permute-start | bytes 393224 | tf_op jit(solution)/shard_map/ppermute | solution.py:344
  75.0 3.1 %shard_map.91 = (bf16[1024,1024]{1,0:T(8,128)(2,1)S(1)}, f32[1024,1024]{1,0:T(8,128)S(1)}) custom-call(s32[8]{0:T(128)S(1)} %get-tuple-element.83.plan, bf16[128,256]{1,0:T(8,128)(2,1)S(1)} %get-tuple-element.113.rest_0_, bf16[128,256]{1,0:T(8,128)(2,1)S(1)} %collective-permute-done.30.rest_1_, bf16[128,256]{1,0:T(8,128)(2,1)S(1)} %collective-permute-done.31.rest_2_, ...), custom_call_target="tpu_custom_call" | custom-call | flops 1073741824 | bytes 2097152 | tf_op jit(solution)/shard_map/pallas_call | solution.py:61
  78.7 9.6 %collective-permute-done.24.rest_5_ = bf16[128,512]{1,0:T(8,128)(2,1)S(1)} collective-permute-done((bf16[128,512]{1,0:T(8,128)(2,1)S(1)}, bf16[128,512]{1,0:T(8,128)(2,1)S(1)}, u32[]{:S(2)}, u32[]{:S(2)}) %collective-permute-start.24) | collective-permute-done | bytes 131104 | tf_op jit(solution)/shard_map/ppermute | solution.py:344
  88.8 2.9 %collective-permute-start.16 = (bf16[128,256]{1,0:T(8,128)(2,1)S(1)}, bf16[128,256]{1,0:T(8,128)(2,1)S(1)}, u32[]{:S(2)}, u32[]{:S(2)}) collective-permute-start(bf16[128,256]{1,0:T(8,128)(2,1)S(1)} %get-tuple-element.96), channel_id=1, source_target_pairs={{0,7},{1,6},{2,5},{3,4},{4,3},{5,2},{6,1},{7,0},{8,15},{9,14},{10,... | collective-permute-start | bytes 196616 | tf_op jit(solution)/shard_map/ppermute | solution.py:344
  91.7 3.2 %shard_map.92 = (bf16[1024,1024]{1,0:T(8,128)(2,1)S(1)}, f32[1024,1024]{1,0:T(8,128)S(1)}) custom-call(s32[8]{0:T(128)S(1)} %get-tuple-element.83.plan, bf16[128,512]{1,0:T(8,128)(2,1)S(1)} %get-tuple-element.101.rest_0_, bf16[128,512]{1,0:T(8,128)(2,1)S(1)} %collective-permute-done.20.rest_1_, ...), custom_call_target="tpu_custom_call", output_to_operand_aliasing={{0}: (11, {}), {1}: (12, {})} | custom-call | flops 2147483648 | bytes 2097152 | tf_op jit(solution)/shard_map/pallas_call | solution.py:61
  94.9 4.6 %collective-permute-done.13.rest_4_ = bf16[128,256]{1,0:T(8,128)(2,1)S(1)} collective-permute-done((bf16[128,256]{1,0:T(8,128)(2,1)S(1)}, bf16[128,256]{1,0:T(8,128)(2,1)S(1)}, u32[]{:S(2)}, u32[]{:S(2)}) %collective-permute-start.13) | collective-permute-done | bytes 65568 | tf_op jit(solution)/shard_map/ppermute | solution.py:344
  99.5 2.1 %collective-permute-done.14.rest_5_ = bf16[128,256]{1,0:T(8,128)(2,1)S(1)} collective-permute-done((bf16[128,256]{1,0:T(8,128)(2,1)S(1)}, bf16[128,256]{1,0:T(8,128)(2,1)S(1)}, u32[]{:S(2)}, u32[]{:S(2)}) %collective-permute-start.14) | collective-permute-done | bytes 65568 | tf_op jit(solution)/shard_map/ppermute | solution.py:344
  101.6 2.4 %shard_map.93 = (bf16[1024,1024]{1,0:T(8,128)(2,1)S(1)}, bf16[1024,256]{1,0:T(8,128)(2,1)S(1)}, bf16[128,512]{1,0:T(8,128)(2,1)S(1)}, bf16[128,512]{1,0:T(8,128)...) custom-call(s32[8]{0:T(128)S(1)} %get-tuple-element.83.plan, ...), custom_call_target="tpu_custom_call", output_to_operand_aliasing={{0}: (13, {})} | custom-call | flops 805306368 | bytes 2097152 | tf_op jit(solution)/shard_map/pallas_call | solution.py:61
  105.3 3.1 %collective-permute-start.58 = (bf16[128,256]{1,0:T(8,128)(2,1)S(1)}, bf16[128,256]{1,0:T(8,128)(2,1)S(1)}, u32[]{:S(2)}, u32[]{:S(2)}) collective-permute-start(bf16[128,256]{1,0:T(8,128)(2,1)S(1)} %get-tuple-element.153), channel_id=1, source_target_pairs={{0,2},{1,3},{2,0},{3,1},{4,6},{5,7},{6,4},{7,5},{8,10},{9,11},{10,... | collective-permute-start | bytes 196616 | tf_op jit(solution)/shard_map/ppermute | solution.py:344
  111.5 1.9 %collective-permute-start.48 = (bf16[128,512]{1,0:T(8,128)(2,1)S(1)}, bf16[128,512]{1,0:T(8,128)(2,1)S(1)}, u32[]{:S(2)}, u32[]{:S(2)}) collective-permute-start(bf16[128,512]{1,0:T(8,128)(2,1)S(1)} %get-tuple-element.141), channel_id=1, source_target_pairs={{0,2},{1,3},{2,0},{3,1},{4,6},{5,7},{6,4},{7,5},{8,10},{9,11},{10,... | collective-permute-start | bytes 393224 | tf_op jit(solution)/shard_map/ppermute | solution.py:344
  113.9 2.2 %collective-permute-start.62 = (bf16[128,256]{1,0:T(8,128)(2,1)S(1)}, bf16[128,256]{1,0:T(8,128)(2,1)S(1)}, u32[]{:S(2)}, u32[]{:S(2)}) collective-permute-start(bf16[128,256]{1,0:T(8,128)(2,1)S(1)} %get-tuple-element.157), channel_id=1, source_target_pairs={{0,6},{1,7},{2,4},{3,5},{4,2},{5,3},{6,0},{7,1},{8,14},{9,15},{10,... | collective-permute-start | bytes 196616 | tf_op jit(solution)/shard_map/ppermute | solution.py:344
  118.1 2.9 %collective-permute-done.62.rest_6_ = bf16[128,256]{1,0:T(8,128)(2,1)S(1)} collective-permute-done((bf16[128,256]{1,0:T(8,128)(2,1)S(1)}, bf16[128,256]{1,0:T(8,128)(2,1)S(1)}, u32[]{:S(2)}, u32[]{:S(2)}) %collective-permute-start.62) | collective-permute-done | bytes 65568 | tf_op jit(solution)/shard_map/ppermute | solution.py:344
  122.4 2.4 %collective-permute-start.50 = (bf16[128,512]{1,0:T(8,128)(2,1)S(1)}, bf16[128,512]{1,0:T(8,128)(2,1)S(1)}, u32[]{:S(2)}, u32[]{:S(2)}) collective-permute-start(bf16[128,512]{1,0:T(8,128)(2,1)S(1)} %get-tuple-element.143), channel_id=1, source_target_pairs={{0,4},{1,5},{2,6},{3,7},{4,0},{5,1},{6,2},{7,3},{8,12},{9,13},{10,... | collective-permute-start | bytes 393224 | tf_op jit(solution)/shard_map/ppermute | solution.py:344
  124.8 1.9 %collective-permute-start.52 = (bf16[128,512]{1,0:T(8,128)(2,1)S(1)}, bf16[128,512]{1,0:T(8,128)(2,1)S(1)}, u32[]{:S(2)}, u32[]{:S(2)}) collective-permute-start(bf16[128,512]{1,0:T(8,128)(2,1)S(1)} %get-tuple-element.145), channel_id=1, source_target_pairs={{0,6},{1,7},{2,4},{3,5},{4,2},{5,3},{6,0},{7,1},{8,14},{9,15},{10,... | collective-permute-start | bytes 393224 | tf_op jit(solution)/shard_map/ppermute | solution.py:344
  128.6 12.3 %collective-permute-done.50.rest_4_ = bf16[128,512]{1,0:T(8,128)(2,1)S(1)} collective-permute-done((bf16[128,512]{1,0:T(8,128)(2,1)S(1)}, bf16[128,512]{1,0:T(8,128)(2,1)S(1)}, u32[]{:S(2)}, u32[]{:S(2)}) %collective-permute-start.50) | collective-permute-done | bytes 131104 | tf_op jit(solution)/shard_map/ppermute | solution.py:344
  143.3 2.6 %collective-permute-start.41 = (bf16[128,256]{1,0:T(8,128)(2,1)S(1)}, bf16[128,256]{1,0:T(8,128)(2,1)S(1)}, u32[]{:S(2)}, u32[]{:S(2)}) collective-permute-start(bf16[128,256]{1,0:T(8,128)(2,1)S(1)} %get-tuple-element.132), channel_id=1, source_target_pairs={{0,5},{1,4},{2,7},{3,6},{4,1},{5,0},{6,3},{7,2},{8,13},{9,12},{10,... | collective-permute-start | bytes 196616 | tf_op jit(solution)/shard_map/ppermute | solution.py:344
  149.8 3.2 %collective-permute-start.43 = (bf16[128,256]{1,0:T(8,128)(2,1)S(1)}, bf16[128,256]{1,0:T(8,128)(2,1)S(1)}, u32[]{:S(2)}, u32[]{:S(2)}) collective-permute-start(bf16[128,256]{1,0:T(8,128)(2,1)S(1)} %get-tuple-element.134), channel_id=1, source_target_pairs={{0,7},{1,6},{2,5},{3,4},{4,3},{5,2},{6,1},{7,0},{8,15},{9,14},{10,... | collective-permute-start | bytes 196616 | tf_op jit(solution)/shard_map/ppermute | solution.py:344
  158.3 5.4 %fusion = f32[1,1024,1024]{2,1,0:T(8,128)} fusion(f32[1,1024,1024]{2,1,0:T(8,128)S(1)} %copy-done.4, bf16[1024,1024]{1,0:T(8,128)(2,1)S(1)} %get-tuple-element.125, f32[]{:T(128)} %bitcast.1), kind=kOutput, calls=%fused_computation.1 | convolution fusion | flops 2150629376 | bytes 10485764 | tf_op jit(solution)/shard_map/dot_general | solution.py:403
  166.1 1.9 %collective-permute-start.46 = (bf16[2,128,256]{2,1,0:T(8,128)(2,1)S(1)}, bf16[2,128,256]{2,1,0:T(8,128)(2,1)S(1)}, u32[]{:S(2)}, u32[]{:S(2)}) collective-permute-start(bf16[2,128,256]{2,1,0:T(8,128)(2,1)S(1)} %get-tuple-element.138), channel_id=1, source_target_pairs={{0,24},{8,16},{16,8},{24,0},{1,25},{9,17},{17,9},{25,1},{2,26},{10... | collective-permute-start | bytes 393224 | tf_op jit(solution)/shard_map/ppermute | solution.py:344
  170.0 5.1 %fusion.1 = f32[1,1024,1024]{2,1,0:T(8,128)} fusion(f32[1,1024,1024]{2,1,0:T(8,128)S(1)} %copy-done.5, bf16[1024,1024]{1,0:T(8,128)(2,1)S(1)} %get-tuple-element.125, f32[]{:T(128)} %bitcast.1), kind=kOutput, calls=%fused_computation.3 | convolution fusion | flops 2150629376 | bytes 10485764 | tf_op jit(solution)/shard_map/dot_general | solution.py:401
  175.1 9.0 %collective-permute-done.55.rest_2_ = bf16[2,128,512]{2,1,0:T(8,128)(2,1)S(1)} collective-permute-done((bf16[2,128,512]{2,1,0:T(8,128)(2,1)S(1)}, bf16[2,128,512]{2,1,0:T(8,128)(2,1)S(1)}, u32[]{:S(2)}, u32[]{:S(2)}) %collective-permute-start.55) | collective-permute-done | bytes 262176 | tf_op jit(solution)/shard_map/ppermute | solution.py:344
  (136 shorter events, 62.5 us)
Async XLA Ops:
  11.7 21.2 %collective-permute-start.27 = (bf16[2,128,256]{2,1,0:T(8,128)(2,1)S(1)}, bf16[2,128,256]{2,1,0:T(8,128)(2,1)S(1)}, u32[]{:S(2)}, u32[]{:S(2)}) collective-permute-start(bf16[2,128,256]{2,1,0:T(8,128)(2,1)S(1)} %get-tuple-element.110), channel_id=1, source_target_pairs={{0,8},{8,0},{16,24},{24,16},{1,9},{9,1},{17,25},{25,17},{2,10},{10... | collective-permute-start | bytes 393224 | tf_op jit(solution)/shard_map/ppermute | solution.py:344
  13.4 20.6 %collective-permute-start.28 = (bf16[2,128,256]{2,1,0:T(8,128)(2,1)S(1)}, bf16[2,128,256]{2,1,0:T(8,128)(2,1)S(1)}, u32[]{:S(2)}, u32[]{:S(2)}) collective-permute-start(bf16[2,128,256]{2,1,0:T(8,128)(2,1)S(1)} %get-tuple-element.111), channel_id=1, source_target_pairs={{0,16},{8,24},{16,0},{24,8},{1,17},{9,25},{17,1},{25,9},{2,18},{10... | collective-permute-start | bytes 393224 | tf_op jit(solution)/shard_map/ppermute | solution.py:344
  16.6 18.8 %collective-permute-start.29 = (bf16[2,128,256]{2,1,0:T(8,128)(2,1)S(1)}, bf16[2,128,256]{2,1,0:T(8,128)(2,1)S(1)}, u32[]{:S(2)}, u32[]{:S(2)}) collective-permute-start(bf16[2,128,256]{2,1,0:T(8,128)(2,1)S(1)} %get-tuple-element.112), channel_id=1, source_target_pairs={{0,24},{8,16},{16,8},{24,0},{1,25},{9,17},{17,9},{25,1},{2,26},{10... | collective-permute-start | bytes 393224 | tf_op jit(solution)/shard_map/ppermute | solution.py:344
  16.9 20.0 %collective-permute-start.7 = (bf16[2,128,256]{2,1,0:T(8,128)(2,1)S(1)}, bf16[2,128,256]{2,1,0:T(8,128)(2,1)S(1)}, u32[]{:S(2)}, u32[]{:S(2)}) collective-permute-start(bf16[2,128,256]{2,1,0:T(8,128)(2,1)S(1)} %get-tuple-element.86), channel_id=1, source_target_pairs={{0,8},{8,0},{16,24},{24,16},{1,9},{9,1},{17,25},{25,17},{2,10},{10... | collective-permute-start | bytes 393224 | tf_op jit(solution)/shard_map/ppermute | solution.py:344
  31.9 18.6 %collective-permute-start.17 = (bf16[2,128,512]{2,1,0:T(8,128)(2,1)S(1)}, bf16[2,128,512]{2,1,0:T(8,128)(2,1)S(1)}, u32[]{:S(2)}, u32[]{:S(2)}) collective-permute-start(bf16[2,128,512]{2,1,0:T(8,128)(2,1)S(1)} %get-tuple-element.98), channel_id=1, source_target_pairs={{0,8},{8,0},{16,24},{24,16},{1,9},{9,1},{17,25},{25,17},{2,10},{10... | collective-permute-start | bytes 786440 | tf_op jit(solution)/shard_map/ppermute | solution.py:344
  32.9 20.8 %collective-permute-start.18 = (bf16[2,128,512]{2,1,0:T(8,128)(2,1)S(1)}, bf16[2,128,512]{2,1,0:T(8,128)(2,1)S(1)}, u32[]{:S(2)}, u32[]{:S(2)}) collective-permute-start(bf16[2,128,512]{2,1,0:T(8,128)(2,1)S(1)} %get-tuple-element.99), channel_id=1, source_target_pairs={{0,16},{8,24},{16,0},{24,8},{1,17},{9,25},{17,1},{25,9},{2,18},{10... | collective-permute-start | bytes 786440 | tf_op jit(solution)/shard_map/ppermute | solution.py:344
  33.9 19.8 %collective-permute-start.19 = (bf16[2,128,512]{2,1,0:T(8,128)(2,1)S(1)}, bf16[2,128,512]{2,1,0:T(8,128)(2,1)S(1)}, u32[]{:S(2)}, u32[]{:S(2)}) collective-permute-start(bf16[2,128,512]{2,1,0:T(8,128)(2,1)S(1)} %get-tuple-element.100), channel_id=1, source_target_pairs={{0,24},{8,16},{16,8},{24,0},{1,25},{9,17},{17,9},{25,1},{2,26},{10... | collective-permute-start | bytes 786440 | tf_op jit(solution)/shard_map/ppermute | solution.py:344
  35.4 13.2 %collective-permute-start.8 = (bf16[2,128,256]{2,1,0:T(8,128)(2,1)S(1)}, bf16[2,128,256]{2,1,0:T(8,128)(2,1)S(1)}, u32[]{:S(2)}, u32[]{:S(2)}) collective-permute-start(bf16[2,128,256]{2,1,0:T(8,128)(2,1)S(1)} %get-tuple-element.87), channel_id=1, source_target_pairs={{0,16},{8,24},{16,0},{24,8},{1,17},{9,25},{17,1},{25,9},{2,18},{10... | collective-permute-start | bytes 393224 | tf_op jit(solution)/shard_map/ppermute | solution.py:344
  57.7 13.2 %collective-permute-start.21 = (bf16[128,512]{1,0:T(8,128)(2,1)S(1)}, bf16[128,512]{1,0:T(8,128)(2,1)S(1)}, u32[]{:S(2)}, u32[]{:S(2)}) collective-permute-start(bf16[128,512]{1,0:T(8,128)(2,1)S(1)} %get-tuple-element.103), channel_id=1, source_target_pairs={{0,2},{1,3},{2,0},{3,1},{4,6},{5,7},{6,4},{7,5},{8,10},{9,11},{10,... | collective-permute-start | bytes 393224 | tf_op jit(solution)/shard_map/ppermute | solution.py:344
  64.8 13.3 %collective-permute-start.22 = (bf16[128,512]{1,0:T(8,128)(2,1)S(1)}, bf16[128,512]{1,0:T(8,128)(2,1)S(1)}, u32[]{:S(2)}, u32[]{:S(2)}) collective-permute-start(bf16[128,512]{1,0:T(8,128)(2,1)S(1)} %get-tuple-element.104), channel_id=1, source_target_pairs={{0,3},{1,2},{2,1},{3,0},{4,7},{5,6},{6,5},{7,4},{8,11},{9,10},{10,... | collective-permute-start | bytes 393224 | tf_op jit(solution)/shard_map/ppermute | solution.py:344
  69.3 19.0 %collective-permute-start.24 = (bf16[128,512]{1,0:T(8,128)(2,1)S(1)}, bf16[128,512]{1,0:T(8,128)(2,1)S(1)}, u32[]{:S(2)}, u32[]{:S(2)}) collective-permute-start(bf16[128,512]{1,0:T(8,128)(2,1)S(1)} %get-tuple-element.106), channel_id=1, source_target_pairs={{0,5},{1,4},{2,7},{3,6},{4,1},{5,0},{6,3},{7,2},{8,13},{9,12},{10,... | collective-permute-start | bytes 393224 | tf_op jit(solution)/shard_map/ppermute | solution.py:344
  70.1 18.2 %collective-permute-start.25 = (bf16[128,512]{1,0:T(8,128)(2,1)S(1)}, bf16[128,512]{1,0:T(8,128)(2,1)S(1)}, u32[]{:S(2)}, u32[]{:S(2)}) collective-permute-start(bf16[128,512]{1,0:T(8,128)(2,1)S(1)} %get-tuple-element.107), channel_id=1, source_target_pairs={{0,6},{1,7},{2,4},{3,5},{4,2},{5,3},{6,0},{7,1},{8,14},{9,15},{10,... | collective-permute-start | bytes 393224 | tf_op jit(solution)/shard_map/ppermute | solution.py:344
  70.8 17.9 %collective-permute-start.26 = (bf16[128,512]{1,0:T(8,128)(2,1)S(1)}, bf16[128,512]{1,0:T(8,128)(2,1)S(1)}, u32[]{:S(2)}, u32[]{:S(2)}) collective-permute-start(bf16[128,512]{1,0:T(8,128)(2,1)S(1)} %get-tuple-element.108), channel_id=1, source_target_pairs={{0,7},{1,6},{2,5},{3,4},{4,3},{5,2},{6,1},{7,0},{8,15},{9,14},{10,... | collective-permute-start | bytes 393224 | tf_op jit(solution)/shard_map/ppermute | solution.py:344
  78.1 16.8 %collective-permute-start.12 = (bf16[128,256]{1,0:T(8,128)(2,1)S(1)}, bf16[128,256]{1,0:T(8,128)(2,1)S(1)}, u32[]{:S(2)}, u32[]{:S(2)}) collective-permute-start(bf16[128,256]{1,0:T(8,128)(2,1)S(1)} %get-tuple-element.92), channel_id=1, source_target_pairs={{0,3},{1,2},{2,1},{3,0},{4,7},{5,6},{6,5},{7,4},{8,11},{9,10},{10,... | collective-permute-start | bytes 196616 | tf_op jit(solution)/shard_map/ppermute | solution.py:344
  78.2 21.4 %collective-permute-start.13 = (bf16[128,256]{1,0:T(8,128)(2,1)S(1)}, bf16[128,256]{1,0:T(8,128)(2,1)S(1)}, u32[]{:S(2)}, u32[]{:S(2)}) collective-permute-start(bf16[128,256]{1,0:T(8,128)(2,1)S(1)} %get-tuple-element.93), channel_id=1, source_target_pairs={{0,4},{1,5},{2,6},{3,7},{4,0},{5,1},{6,2},{7,3},{8,12},{9,13},{10,... | collective-permute-start | bytes 196616 | tf_op jit(solution)/shard_map/ppermute | solution.py:344
  88.3 13.3 %collective-permute-start.14 = (bf16[128,256]{1,0:T(8,128)(2,1)S(1)}, bf16[128,256]{1,0:T(8,128)(2,1)S(1)}, u32[]{:S(2)}, u32[]{:S(2)}) collective-permute-start(bf16[128,256]{1,0:T(8,128)(2,1)S(1)} %get-tuple-element.94), channel_id=1, source_target_pairs={{0,5},{1,4},{2,7},{3,6},{4,1},{5,0},{6,3},{7,2},{8,13},{9,12},{10,... | collective-permute-start | bytes 196616 | tf_op jit(solution)/shard_map/ppermute | solution.py:344
  88.3 13.3 %collective-permute-start.15 = (bf16[128,256]{1,0:T(8,128)(2,1)S(1)}, bf16[128,256]{1,0:T(8,128)(2,1)S(1)}, u32[]{:S(2)}, u32[]{:S(2)}) collective-permute-start(bf16[128,256]{1,0:T(8,128)(2,1)S(1)} %get-tuple-element.95), channel_id=1, source_target_pairs={{0,6},{1,7},{2,4},{3,5},{4,2},{5,3},{6,0},{7,1},{8,14},{9,15},{10,... | collective-permute-start | bytes 196616 | tf_op jit(solution)/shard_map/ppermute | solution.py:344
  88.8 12.8 %collective-permute-start.16 = (bf16[128,256]{1,0:T(8,128)(2,1)S(1)}, bf16[128,256]{1,0:T(8,128)(2,1)S(1)}, u32[]{:S(2)}, u32[]{:S(2)}) collective-permute-start(bf16[128,256]{1,0:T(8,128)(2,1)S(1)} %get-tuple-element.96), channel_id=1, source_target_pairs={{0,7},{1,6},{2,5},{3,4},{4,3},{5,2},{6,1},{7,0},{8,15},{9,14},{10,... | collective-permute-start | bytes 196616 | tf_op jit(solution)/shard_map/ppermute | solution.py:344
  110.9 13.9 %collective-permute-start.47 = (bf16[128,512]{1,0:T(8,128)(2,1)S(1)}, bf16[128,512]{1,0:T(8,128)(2,1)S(1)}, u32[]{:S(2)}, u32[]{:S(2)}) collective-permute-start(bf16[128,512]{1,0:T(8,128)(2,1)S(1)} %get-tuple-element.140), channel_id=1, source_target_pairs={{0,1},{1,0},{2,3},{3,2},{4,5},{5,4},{6,7},{7,6},{8,9},{9,8},{10,11... | collective-permute-start | bytes 393224 | tf_op jit(solution)/shard_map/ppermute | solution.py:344
  111.5 15.2 %collective-permute-start.48 = (bf16[128,512]{1,0:T(8,128)(2,1)S(1)}, bf16[128,512]{1,0:T(8,128)(2,1)S(1)}, u32[]{:S(2)}, u32[]{:S(2)}) collective-permute-start(bf16[128,512]{1,0:T(8,128)(2,1)S(1)} %get-tuple-element.141), channel_id=1, source_target_pairs={{0,2},{1,3},{2,0},{3,1},{4,6},{5,7},{6,4},{7,5},{8,10},{9,11},{10,... | collective-permute-start | bytes 393224 | tf_op jit(solution)/shard_map/ppermute | solution.py:344
  122.4 18.5 %collective-permute-start.50 = (bf16[128,512]{1,0:T(8,128)(2,1)S(1)}, bf16[128,512]{1,0:T(8,128)(2,1)S(1)}, u32[]{:S(2)}, u32[]{:S(2)}) collective-permute-start(bf16[128,512]{1,0:T(8,128)(2,1)S(1)} %get-tuple-element.143), channel_id=1, source_target_pairs={{0,4},{1,5},{2,6},{3,7},{4,0},{5,1},{6,2},{7,3},{8,12},{9,13},{10,... | collective-permute-start | bytes 393224 | tf_op jit(solution)/shard_map/ppermute | solution.py:344
  124.8 17.2 %collective-permute-start.51 = (bf16[128,512]{1,0:T(8,128)(2,1)S(1)}, bf16[128,512]{1,0:T(8,128)(2,1)S(1)}, u32[]{:S(2)}, u32[]{:S(2)}) collective-permute-start(bf16[128,512]{1,0:T(8,128)(2,1)S(1)} %get-tuple-element.144), channel_id=1, source_target_pairs={{0,5},{1,4},{2,7},{3,6},{4,1},{5,0},{6,3},{7,2},{8,13},{9,12},{10,... | collective-permute-start | bytes 393224 | tf_op jit(solution)/shard_map/ppermute | solution.py:344
  124.8 18.5 %collective-permute-start.52 = (bf16[128,512]{1,0:T(8,128)(2,1)S(1)}, bf16[128,512]{1,0:T(8,128)(2,1)S(1)}, u32[]{:S(2)}, u32[]{:S(2)}) collective-permute-start(bf16[128,512]{1,0:T(8,128)(2,1)S(1)} %get-tuple-element.145), channel_id=1, source_target_pairs={{0,6},{1,7},{2,4},{3,5},{4,2},{5,3},{6,0},{7,1},{8,14},{9,15},{10,... | collective-permute-start | bytes 393224 | tf_op jit(solution)/shard_map/ppermute | solution.py:344
  126.7 19.2 %collective-permute-start.53 = (bf16[128,512]{1,0:T(8,128)(2,1)S(1)}, bf16[128,512]{1,0:T(8,128)(2,1)S(1)}, u32[]{:S(2)}, u32[]{:S(2)}) collective-permute-start(bf16[128,512]{1,0:T(8,128)(2,1)S(1)} %get-tuple-element.146), channel_id=1, source_target_pairs={{0,7},{1,6},{2,5},{3,4},{4,3},{5,2},{6,1},{7,0},{8,15},{9,14},{10,... | collective-permute-start | bytes 393224 | tf_op jit(solution)/shard_map/ppermute | solution.py:344
  128.6 21.2 %collective-permute-start.38 = (bf16[128,256]{1,0:T(8,128)(2,1)S(1)}, bf16[128,256]{1,0:T(8,128)(2,1)S(1)}, u32[]{:S(2)}, u32[]{:S(2)}) collective-permute-start(bf16[128,256]{1,0:T(8,128)(2,1)S(1)} %get-tuple-element.129), channel_id=1, source_target_pairs={{0,2},{1,3},{2,0},{3,1},{4,6},{5,7},{6,4},{7,5},{8,10},{9,11},{10,... | collective-permute-start | bytes 196616 | tf_op jit(solution)/shard_map/ppermute | solution.py:344
  141.9 12.9 %collective-permute-start.40 = (bf16[128,256]{1,0:T(8,128)(2,1)S(1)}, bf16[128,256]{1,0:T(8,128)(2,1)S(1)}, u32[]{:S(2)}, u32[]{:S(2)}) collective-permute-start(bf16[128,256]{1,0:T(8,128)(2,1)S(1)} %get-tuple-element.131), channel_id=1, source_target_pairs={{0,4},{1,5},{2,6},{3,7},{4,0},{5,1},{6,2},{7,3},{8,12},{9,13},{10,... | collective-permute-start | bytes 196616 | tf_op jit(solution)/shard_map/ppermute | solution.py:344
  149.8 13.8 %collective-permute-start.43 = (bf16[128,256]{1,0:T(8,128)(2,1)S(1)}, bf16[128,256]{1,0:T(8,128)(2,1)S(1)}, u32[]{:S(2)}, u32[]{:S(2)}) collective-permute-start(bf16[128,256]{1,0:T(8,128)(2,1)S(1)} %get-tuple-element.134), channel_id=1, source_target_pairs={{0,7},{1,6},{2,5},{3,4},{4,3},{5,2},{6,1},{7,0},{8,15},{9,14},{10,... | collective-permute-start | bytes 196616 | tf_op jit(solution)/shard_map/ppermute | solution.py:344
  164.4 21.5 %collective-permute-start.44 = (bf16[2,128,256]{2,1,0:T(8,128)(2,1)S(1)}, bf16[2,128,256]{2,1,0:T(8,128)(2,1)S(1)}, u32[]{:S(2)}, u32[]{:S(2)}) collective-permute-start(bf16[2,128,256]{2,1,0:T(8,128)(2,1)S(1)} %get-tuple-element.136), channel_id=1, source_target_pairs={{0,8},{8,0},{16,24},{24,16},{1,9},{9,1},{17,25},{25,17},{2,10},{10... | collective-permute-start | bytes 393224 | tf_op jit(solution)/shard_map/ppermute | solution.py:344
  165.0 20.9 %collective-permute-start.45 = (bf16[2,128,256]{2,1,0:T(8,128)(2,1)S(1)}, bf16[2,128,256]{2,1,0:T(8,128)(2,1)S(1)}, u32[]{:S(2)}, u32[]{:S(2)}) collective-permute-start(bf16[2,128,256]{2,1,0:T(8,128)(2,1)S(1)} %get-tuple-element.137), channel_id=1, source_target_pairs={{0,16},{8,24},{16,0},{24,8},{1,17},{9,25},{17,1},{25,9},{2,18},{10... | collective-permute-start | bytes 393224 | tf_op jit(solution)/shard_map/ppermute | solution.py:344
  166.1 19.8 %collective-permute-start.46 = (bf16[2,128,256]{2,1,0:T(8,128)(2,1)S(1)}, bf16[2,128,256]{2,1,0:T(8,128)(2,1)S(1)}, u32[]{:S(2)}, u32[]{:S(2)}) collective-permute-start(bf16[2,128,256]{2,1,0:T(8,128)(2,1)S(1)} %get-tuple-element.138), channel_id=1, source_target_pairs={{0,24},{8,16},{16,8},{24,0},{1,25},{9,17},{17,9},{25,1},{2,26},{10... | collective-permute-start | bytes 393224 | tf_op jit(solution)/shard_map/ppermute | solution.py:344
  168.0 16.1 %collective-permute-start.55 = (bf16[2,128,512]{2,1,0:T(8,128)(2,1)S(1)}, bf16[2,128,512]{2,1,0:T(8,128)(2,1)S(1)}, u32[]{:S(2)}, u32[]{:S(2)}) collective-permute-start(bf16[2,128,512]{2,1,0:T(8,128)(2,1)S(1)} %get-tuple-element.149), channel_id=1, source_target_pairs={{0,16},{8,24},{16,0},{24,8},{1,17},{9,25},{17,1},{25,9},{2,18},{10... | collective-permute-start | bytes 786440 | tf_op jit(solution)/shard_map/ppermute | solution.py:344
  168.6 15.5 %collective-permute-start.56 = (bf16[2,128,512]{2,1,0:T(8,128)(2,1)S(1)}, bf16[2,128,512]{2,1,0:T(8,128)(2,1)S(1)}, u32[]{:S(2)}, u32[]{:S(2)}) collective-permute-start(bf16[2,128,512]{2,1,0:T(8,128)(2,1)S(1)} %get-tuple-element.150), channel_id=1, source_target_pairs={{0,24},{8,16},{16,8},{24,0},{1,25},{9,17},{17,9},{25,1},{2,26},{10... | collective-permute-start | bytes 786440 | tf_op jit(solution)/shard_map/ppermute | solution.py:344
  (41 other events, 517.2 us)

commit v3 on v2

--- a/solution.py
+++ b/solution.py
@@ -252,7 +252,7 @@
         block, total = rest[-2:]
         gather(pieces, block, mp, at, width)
 
-        @pl.loop(0, blk // tile)
+        @pl.loop(0, blk // tile, unroll=True)
         def _(i):
             span = pl.ds(pl.multiple_of(i * tile, tile), tile)
             half = jnp.dot(left[span, :], block[:, at : at + width], preferred_element_type=jnp.float32)
@@ -281,7 +281,7 @@
 def last_update(pieces, left_root, right_root, block, total, scale, plan, mp, at, width, cut):
     rows = pieces[0].shape[0]
     blk = left_root.shape[0]
-    tile = min(512, blk)
+    tile = blk
     start, size = cut
 
     def body(plan, *rest):
@@ -291,7 +291,7 @@
         gather(pieces, block, mp, at, width)
         scaling = scale[0:1, 0:1]
 
-        @pl.loop(0, blk // tile)
+        @pl.loop(0, blk // tile, unroll=True)
         def _(i):
             span = pl.ds(pl.multiple_of(i * tile, tile), tile)
             term = jnp.dot(left[span, :], block[:, at : at + width], preferred_element_type=jnp.float32)
@@ -324,7 +324,7 @@
         outs, update = rest[:-1], rest[-1]
         scaling = scale[0:1, 0:1]
 
-        @pl.loop(0, blk // tile)
+        @pl.loop(0, blk // tile, unroll=True)
         def _(i):
             span = pl.ds(pl.multiple_of(i * tile, tile), tile)
             term = jnp.dot(half[span, :], right[at : at + width, base:], preferred_element_type=jnp.float32)

time: 188 us -> 187 us (level)
  no operation moved by 1% of the time
where the time goes in v3:
time: 187 us
  starting transfers between devices  79.8 us (43%)
  waiting for transfers between devices  70.3 us (38%)
  Pallas kernels  23.3 us (12%)
  matrix products  10.5 us (6%)
  local copies, waits for them, and re-layouts  2.12 us (1%)
    ppermute x67, starting transfers between devices, swap(): return lax.ppermute(value, axis, [(i, i ^ distance) for i in range(count)])  79.8 us
    ppermute x67, waiting for transfers between devices, swap(): return lax.ppermute(value, axis, [(i, i ^ distance) for i in range(count)])  70.3 us
    pallas_call x15, Pallas kernels, call(): pl.pallas_call(body, out_shape=outs, in_specs=[SMEM] + ins, out_specs=out...  21.5 us
    dot_general x1, matrix products, per_device(): right_gram = jnp.dot(block.T, block, preferred_element_type=jnp.float32)  5.37 us
    dot_general x1, matrix products, per_device(): left_gram = jnp.dot(block, block.T, preferred_element_type=jnp.float32)  5.08 us
  transfers between devices with their start and end apart: 67, of which 19 were waited for; matrix products, arithmetic and copies ran while one was open for 6% of the time, Pallas kernels for 9%

profile of v3, /device:TPU:0, one launch (start us, length us, event | category | flops | bytes accessed | tf_op | source)
XLA Modules:
  0.0 187.0 jit_solution(1633794354554076048)
XLA Ops:
  6.2 2.9 %collective-permute-start.1 = (f32[8,128]{1,0:T(8,128)S(1)}, f32[8,128]{1,0:T(8,128)S(1)}, u32[]{:S(2)}, u32[]{:S(2)}) collective-permute-start(f32[8,128]{1,0:T(8,128)S(1)} %add.33), channel_id=1, source_target_pairs={{0,2},{1,3},{2,0},{3,1},{4,6},{5,7},{6,4},{7,5},{8,10},{9,11},{10,... | collective-permute-start | bytes 12296 | tf_op jit(solution)/shard_map/ppermute | solution.py:344
  9.1 2.6 %collective-permute-start.2 = (f32[8,128]{1,0:T(8,128)S(1)}, f32[8,128]{1,0:T(8,128)S(1)}, u32[]{:S(2)}, u32[]{:S(2)}) collective-permute-start(f32[8,128]{1,0:T(8,128)S(1)} %add.33), channel_id=1, source_target_pairs={{0,4},{1,5},{2,6},{3,7},{4,0},{5,1},{6,2},{7,3},{8,12},{9,13},{10,... | collective-permute-start | bytes 12296 | tf_op jit(solution)/shard_map/ppermute | solution.py:344
  19.0 4.8 %collective-permute-done.4 = f32[8,128]{1,0:T(8,128)S(1)} collective-permute-done((f32[8,128]{1,0:T(8,128)S(1)}, f32[8,128]{1,0:T(8,128)S(1)}, u32[]{:S(2)}, u32[]{:S(2)}) %collective-permute-start.4) | collective-permute-done | bytes 4128 | tf_op jit(solution)/shard_map/ppermute | solution.py:344
  25.2 2.1 %collective-permute-done.5 = f32[8,128]{1,0:T(8,128)S(1)} collective-permute-done((f32[8,128]{1,0:T(8,128)S(1)}, f32[8,128]{1,0:T(8,128)S(1)}, u32[]{:S(2)}, u32[]{:S(2)}) %collective-permute-start.5) | collective-permute-done | bytes 4128 | tf_op jit(solution)/shard_map/ppermute | solution.py:344
  28.8 2.5 %shard_map.86 = (bf16[2,128,512]{2,1,0:T(8,128)(2,1)S(1)}, bf16[2,128,512]{2,1,0:T(8,128)(2,1)S(1)}, bf16[2,128,512]{2,1,0:T(8,128)(2,1)S(1)}, bf16[2,128,512]{2,1,0:T(8,128)(2,1)S(1)}, s32[8]{0:T(128)S(1)}) custom-call(s32[8]{0:T(128)S(1)} %get-tuple-element.83.plan, bf16[128,8192]{1,0:T(8,128)(2,1)} %grad.7, s32[32]{0:T(128)S(1)} %copy-done.3), custom_call_target="tpu_custom_call" | custom-call | bytes 2097152 | tf_op jit(solution)/shard_map/pallas_call | solution.py:61
  38.6 10.0 %collective-permute-done.8.rest_2_ = bf16[2,128,256]{2,1,0:T(8,128)(2,1)S(1)} collective-permute-done((bf16[2,128,256]{2,1,0:T(8,128)(2,1)S(1)}, bf16[2,128,256]{2,1,0:T(8,128)(2,1)S(1)}, u32[]{:S(2)}, u32[]{:S(2)}) %collective-permute-start.8) | collective-permute-done | bytes 131104 | tf_op jit(solution)/shard_map/ppermute | solution.py:344
  50.5 3.2 %collective-permute-start.33 = (bf16[128,256]{1,0:T(8,128)(2,1)S(1)}, bf16[128,256]{1,0:T(8,128)(2,1)S(1)}, u32[]{:S(2)}, u32[]{:S(2)}) collective-permute-start(bf16[128,256]{1,0:T(8,128)(2,1)S(1)} %get-tuple-element.117), channel_id=1, source_target_pairs={{0,4},{1,5},{2,6},{3,7},{4,0},{5,1},{6,2},{7,3},{8,12},{9,13},{10,... | collective-permute-start | bytes 196616 | tf_op jit(solution)/shard_map/ppermute | solution.py:344
  53.8 2.8 %collective-permute-start.35 = (bf16[128,256]{1,0:T(8,128)(2,1)S(1)}, bf16[128,256]{1,0:T(8,128)(2,1)S(1)}, u32[]{:S(2)}, u32[]{:S(2)}) collective-permute-start(bf16[128,256]{1,0:T(8,128)(2,1)S(1)} %get-tuple-element.119), channel_id=1, source_target_pairs={{0,6},{1,7},{2,4},{3,5},{4,2},{5,3},{6,0},{7,1},{8,14},{9,15},{10,... | collective-permute-start | bytes 196616 | tf_op jit(solution)/shard_map/ppermute | solution.py:344
  59.5 2.8 %collective-permute-done.34.rest_5_ = bf16[128,256]{1,0:T(8,128)(2,1)S(1)} collective-permute-done((bf16[128,256]{1,0:T(8,128)(2,1)S(1)}, bf16[128,256]{1,0:T(8,128)(2,1)S(1)}, u32[]{:S(2)}, u32[]{:S(2)}) %collective-permute-start.34) | collective-permute-done | bytes 65568 | tf_op jit(solution)/shard_map/ppermute | solution.py:344
  62.2 2.1 %collective-permute-start.10 = (bf16[128,256]{1,0:T(8,128)(2,1)S(1)}, bf16[128,256]{1,0:T(8,128)(2,1)S(1)}, u32[]{:S(2)}, u32[]{:S(2)}) collective-permute-start(bf16[128,256]{1,0:T(8,128)(2,1)S(1)} %get-tuple-element.90), channel_id=1, source_target_pairs={{0,1},{1,0},{2,3},{3,2},{4,5},{5,4},{6,7},{7,6},{8,9},{9,8},{10,11... | collective-permute-start | bytes 196616 | tf_op jit(solution)/shard_map/ppermute | solution.py:344
  66.8 2.4 %collective-permute-done.11.rest_2_ = bf16[128,256]{1,0:T(8,128)(2,1)S(1)} collective-permute-done((bf16[128,256]{1,0:T(8,128)(2,1)S(1)}, bf16[128,256]{1,0:T(8,128)(2,1)S(1)}, u32[]{:S(2)}, u32[]{:S(2)}) %collective-permute-start.11) | collective-permute-done | bytes 65568 | tf_op jit(solution)/shard_map/ppermute | solution.py:344
  70.8 4.1 %collective-permute-start.26 = (bf16[128,512]{1,0:T(8,128)(2,1)S(1)}, bf16[128,512]{1,0:T(8,128)(2,1)S(1)}, u32[]{:S(2)}, u32[]{:S(2)}) collective-permute-start(bf16[128,512]{1,0:T(8,128)(2,1)S(1)} %get-tuple-element.108), channel_id=1, source_target_pairs={{0,7},{1,6},{2,5},{3,4},{4,3},{5,2},{6,1},{7,0},{8,15},{9,14},{10,... | collective-permute-start | bytes 393224 | tf_op jit(solution)/shard_map/ppermute | solution.py:344
  75.0 2.4 %shard_map.91 = (bf16[1024,1024]{1,0:T(8,128)(2,1)S(1)}, f32[1024,1024]{1,0:T(8,128)S(1)}) custom-call(s32[8]{0:T(128)S(1)} %get-tuple-element.83.plan, bf16[128,256]{1,0:T(8,128)(2,1)S(1)} %get-tuple-element.113.rest_0_, bf16[128,256]{1,0:T(8,128)(2,1)S(1)} %collective-permute-done.30.rest_1_, bf16[128,256]{1,0:T(8,128)(2,1)S(1)} %collective-permute-done.31.rest_2_, ...), custom_call_target="tpu_custom_call" | custom-call | flops 1073741824 | bytes 2097152 | tf_op jit(solution)/shard_map/pallas_call | solution.py:61
  78.0 10.2 %collective-permute-done.24.rest_5_ = bf16[128,512]{1,0:T(8,128)(2,1)S(1)} collective-permute-done((bf16[128,512]{1,0:T(8,128)(2,1)S(1)}, bf16[128,512]{1,0:T(8,128)(2,1)S(1)}, u32[]{:S(2)}, u32[]{:S(2)}) %collective-permute-start.24) | collective-permute-done | bytes 131104 | tf_op jit(solution)/shard_map/ppermute | solution.py:344
  88.8 2.9 %collective-permute-start.16 = (bf16[128,256]{1,0:T(8,128)(2,1)S(1)}, bf16[128,256]{1,0:T(8,128)(2,1)S(1)}, u32[]{:S(2)}, u32[]{:S(2)}) collective-permute-start(bf16[128,256]{1,0:T(8,128)(2,1)S(1)} %get-tuple-element.96), channel_id=1, source_target_pairs={{0,7},{1,6},{2,5},{3,4},{4,3},{5,2},{6,1},{7,0},{8,15},{9,14},{10,... | collective-permute-start | bytes 196616 | tf_op jit(solution)/shard_map/ppermute | solution.py:344
  91.7 3.0 %shard_map.92 = (bf16[1024,1024]{1,0:T(8,128)(2,1)S(1)}, f32[1024,1024]{1,0:T(8,128)S(1)}) custom-call(s32[8]{0:T(128)S(1)} %get-tuple-element.83.plan, bf16[128,512]{1,0:T(8,128)(2,1)S(1)} %get-tuple-element.101.rest_0_, bf16[128,512]{1,0:T(8,128)(2,1)S(1)} %collective-permute-done.20.rest_1_, ...), custom_call_target="tpu_custom_call", output_to_operand_aliasing={{0}: (11, {}), {1}: (12, {})} | custom-call | flops 2147483648 | bytes 2097152 | tf_op jit(solution)/shard_map/pallas_call | solution.py:61
  94.7 4.8 %collective-permute-done.13.rest_4_ = bf16[128,256]{1,0:T(8,128)(2,1)S(1)} collective-permute-done((bf16[128,256]{1,0:T(8,128)(2,1)S(1)}, bf16[128,256]{1,0:T(8,128)(2,1)S(1)}, u32[]{:S(2)}, u32[]{:S(2)}) %collective-permute-start.13) | collective-permute-done | bytes 65568 | tf_op jit(solution)/shard_map/ppermute | solution.py:344
  99.5 2.1 %collective-permute-done.14.rest_5_ = bf16[128,256]{1,0:T(8,128)(2,1)S(1)} collective-permute-done((bf16[128,256]{1,0:T(8,128)(2,1)S(1)}, bf16[128,256]{1,0:T(8,128)(2,1)S(1)}, u32[]{:S(2)}, u32[]{:S(2)}) %collective-permute-start.14) | collective-permute-done | bytes 65568 | tf_op jit(solution)/shard_map/ppermute | solution.py:344
  101.6 2.1 %shard_map.93 = (bf16[1024,1024]{1,0:T(8,128)(2,1)S(1)}, bf16[1024,256]{1,0:T(8,128)(2,1)S(1)}, bf16[128,512]{1,0:T(8,128)(2,1)S(1)}, bf16[128,512]{1,0:T(8,128)...) custom-call(s32[8]{0:T(128)S(1)} %get-tuple-element.83.plan, ...), custom_call_target="tpu_custom_call", output_to_operand_aliasing={{0}: (13, {})} | custom-call | flops 805306368 | bytes 2097152 | tf_op jit(solution)/shard_map/pallas_call | solution.py:61
  104.9 3.1 %collective-permute-start.58 = (bf16[128,256]{1,0:T(8,128)(2,1)S(1)}, bf16[128,256]{1,0:T(8,128)(2,1)S(1)}, u32[]{:S(2)}, u32[]{:S(2)}) collective-permute-start(bf16[128,256]{1,0:T(8,128)(2,1)S(1)} %get-tuple-element.153), channel_id=1, source_target_pairs={{0,2},{1,3},{2,0},{3,1},{4,6},{5,7},{6,4},{7,5},{8,10},{9,11},{10,... | collective-permute-start | bytes 196616 | tf_op jit(solution)/shard_map/ppermute | solution.py:344
  111.1 1.9 %collective-permute-start.48 = (bf16[128,512]{1,0:T(8,128)(2,1)S(1)}, bf16[128,512]{1,0:T(8,128)(2,1)S(1)}, u32[]{:S(2)}, u32[]{:S(2)}) collective-permute-start(bf16[128,512]{1,0:T(8,128)(2,1)S(1)} %get-tuple-element.141), channel_id=1, source_target_pairs={{0,2},{1,3},{2,0},{3,1},{4,6},{5,7},{6,4},{7,5},{8,10},{9,11},{10,... | collective-permute-start | bytes 393224 | tf_op jit(solution)/shard_map/ppermute | solution.py:344
  113.4 2.2 %collective-permute-start.62 = (bf16[128,256]{1,0:T(8,128)(2,1)S(1)}, bf16[128,256]{1,0:T(8,128)(2,1)S(1)}, u32[]{:S(2)}, u32[]{:S(2)}) collective-permute-start(bf16[128,256]{1,0:T(8,128)(2,1)S(1)} %get-tuple-element.157), channel_id=1, source_target_pairs={{0,6},{1,7},{2,4},{3,5},{4,2},{5,3},{6,0},{7,1},{8,14},{9,15},{10,... | collective-permute-start | bytes 196616 | tf_op jit(solution)/shard_map/ppermute | solution.py:344
  117.6 2.9 %collective-permute-done.62.rest_6_ = bf16[128,256]{1,0:T(8,128)(2,1)S(1)} collective-permute-done((bf16[128,256]{1,0:T(8,128)(2,1)S(1)}, bf16[128,256]{1,0:T(8,128)(2,1)S(1)}, u32[]{:S(2)}, u32[]{:S(2)}) %collective-permute-start.62) | collective-permute-done | bytes 65568 | tf_op jit(solution)/shard_map/ppermute | solution.py:344
  121.9 2.4 %collective-permute-start.50 = (bf16[128,512]{1,0:T(8,128)(2,1)S(1)}, bf16[128,512]{1,0:T(8,128)(2,1)S(1)}, u32[]{:S(2)}, u32[]{:S(2)}) collective-permute-start(bf16[128,512]{1,0:T(8,128)(2,1)S(1)} %get-tuple-element.143), channel_id=1, source_target_pairs={{0,4},{1,5},{2,6},{3,7},{4,0},{5,1},{6,2},{7,3},{8,12},{9,13},{10,... | collective-permute-start | bytes 393224 | tf_op jit(solution)/shard_map/ppermute | solution.py:344
  124.3 1.9 %collective-permute-start.52 = (bf16[128,512]{1,0:T(8,128)(2,1)S(1)}, bf16[128,512]{1,0:T(8,128)(2,1)S(1)}, u32[]{:S(2)}, u32[]{:S(2)}) collective-permute-start(bf16[128,512]{1,0:T(8,128)(2,1)S(1)} %get-tuple-element.145), channel_id=1, source_target_pairs={{0,6},{1,7},{2,4},{3,5},{4,2},{5,3},{6,0},{7,1},{8,14},{9,15},{10,... | collective-permute-start | bytes 393224 | tf_op jit(solution)/shard_map/ppermute | solution.py:344
  128.1 12.3 %collective-permute-done.50.rest_4_ = bf16[128,512]{1,0:T(8,128)(2,1)S(1)} collective-permute-done((bf16[128,512]{1,0:T(8,128)(2,1)S(1)}, bf16[128,512]{1,0:T(8,128)(2,1)S(1)}, u32[]{:S(2)}, u32[]{:S(2)}) %collective-permute-start.50) | collective-permute-done | bytes 131104 | tf_op jit(solution)/shard_map/ppermute | solution.py:344
  142.8 2.6 %collective-permute-start.41 = (bf16[128,256]{1,0:T(8,128)(2,1)S(1)}, bf16[128,256]{1,0:T(8,128)(2,1)S(1)}, u32[]{:S(2)}, u32[]{:S(2)}) collective-permute-start(bf16[128,256]{1,0:T(8,128)(2,1)S(1)} %get-tuple-element.132), channel_id=1, source_target_pairs={{0,5},{1,4},{2,7},{3,6},{4,1},{5,0},{6,3},{7,2},{8,13},{9,12},{10,... | collective-permute-start | bytes 196616 | tf_op jit(solution)/shard_map/ppermute | solution.py:344
  149.3 3.2 %collective-permute-start.43 = (bf16[128,256]{1,0:T(8,128)(2,1)S(1)}, bf16[128,256]{1,0:T(8,128)(2,1)S(1)}, u32[]{:S(2)}, u32[]{:S(2)}) collective-permute-start(bf16[128,256]{1,0:T(8,128)(2,1)S(1)} %get-tuple-element.134), channel_id=1, source_target_pairs={{0,7},{1,6},{2,5},{3,4},{4,3},{5,2},{6,1},{7,0},{8,15},{9,14},{10,... | collective-permute-start | bytes 196616 | tf_op jit(solution)/shard_map/ppermute | solution.py:344
  157.8 5.4 %fusion = f32[1,1024,1024]{2,1,0:T(8,128)} fusion(f32[1,1024,1024]{2,1,0:T(8,128)S(1)} %copy-done.4, bf16[1024,1024]{1,0:T(8,128)(2,1)S(1)} %get-tuple-element.125, f32[]{:T(128)} %bitcast.1), kind=kOutput, calls=%fused_computation.1 | convolution fusion | flops 2150629376 | bytes 10485764 | tf_op jit(solution)/shard_map/dot_general | solution.py:403
  165.6 1.9 %collective-permute-start.46 = (bf16[2,128,256]{2,1,0:T(8,128)(2,1)S(1)}, bf16[2,128,256]{2,1,0:T(8,128)(2,1)S(1)}, u32[]{:S(2)}, u32[]{:S(2)}) collective-permute-start(bf16[2,128,256]{2,1,0:T(8,128)(2,1)S(1)} %get-tuple-element.138), channel_id=1, source_target_pairs={{0,24},{8,16},{16,8},{24,0},{1,25},{9,17},{17,9},{25,1},{2,26},{10... | collective-permute-start | bytes 393224 | tf_op jit(solution)/shard_map/ppermute | solution.py:344
  169.5 5.1 %fusion.1 = f32[1,1024,1024]{2,1,0:T(8,128)} fusion(f32[1,1024,1024]{2,1,0:T(8,128)S(1)} %copy-done.5, bf16[1024,1024]{1,0:T(8,128)(2,1)S(1)} %get-tuple-element.125, f32[]{:T(128)} %bitcast.1), kind=kOutput, calls=%fused_computation.3 | convolution fusion | flops 2150629376 | bytes 10485764 | tf_op jit(solution)/shard_map/dot_general | solution.py:401
  174.6 9.0 %collective-permute-done.55.rest_2_ = bf16[2,128,512]{2,1,0:T(8,128)(2,1)S(1)} collective-permute-done((bf16[2,128,512]{2,1,0:T(8,128)(2,1)S(1)}, bf16[2,128,512]{2,1,0:T(8,128)(2,1)S(1)}, u32[]{:S(2)}, u32[]{:S(2)}) %collective-permute-start.55) | collective-permute-done | bytes 262176 | tf_op jit(solution)/shard_map/ppermute | solution.py:344
  (136 shorter events, 62.3 us)
Async XLA Ops:
  11.7 21.2 %collective-permute-start.27 = (bf16[2,128,256]{2,1,0:T(8,128)(2,1)S(1)}, bf16[2,128,256]{2,1,0:T(8,128)(2,1)S(1)}, u32[]{:S(2)}, u32[]{:S(2)}) collective-permute-start(bf16[2,128,256]{2,1,0:T(8,128)(2,1)S(1)} %get-tuple-element.110), channel_id=1, source_target_pairs={{0,8},{8,0},{16,24},{24,16},{1,9},{9,1},{17,25},{25,17},{2,10},{10... | collective-permute-start | bytes 393224 | tf_op jit(solution)/shard_map/ppermute | solution.py:344
  13.4 20.6 %collective-permute-start.28 = (bf16[2,128,256]{2,1,0:T(8,128)(2,1)S(1)}, bf16[2,128,256]{2,1,0:T(8,128)(2,1)S(1)}, u32[]{:S(2)}, u32[]{:S(2)}) collective-permute-start(bf16[2,128,256]{2,1,0:T(8,128)(2,1)S(1)} %get-tuple-element.111), channel_id=1, source_target_pairs={{0,16},{8,24},{16,0},{24,8},{1,17},{9,25},{17,1},{25,9},{2,18},{10... | collective-permute-start | bytes 393224 | tf_op jit(solution)/shard_map/ppermute | solution.py:344
  16.6 18.8 %collective-permute-start.29 = (bf16[2,128,256]{2,1,0:T(8,128)(2,1)S(1)}, bf16[2,128,256]{2,1,0:T(8,128)(2,1)S(1)}, u32[]{:S(2)}, u32[]{:S(2)}) collective-permute-start(bf16[2,128,256]{2,1,0:T(8,128)(2,1)S(1)} %get-tuple-element.112), channel_id=1, source_target_pairs={{0,24},{8,16},{16,8},{24,0},{1,25},{9,17},{17,9},{25,1},{2,26},{10... | collective-permute-start | bytes 393224 | tf_op jit(solution)/shard_map/ppermute | solution.py:344
  16.9 20.0 %collective-permute-start.7 = (bf16[2,128,256]{2,1,0:T(8,128)(2,1)S(1)}, bf16[2,128,256]{2,1,0:T(8,128)(2,1)S(1)}, u32[]{:S(2)}, u32[]{:S(2)}) collective-permute-start(bf16[2,128,256]{2,1,0:T(8,128)(2,1)S(1)} %get-tuple-element.86), channel_id=1, source_target_pairs={{0,8},{8,0},{16,24},{24,16},{1,9},{9,1},{17,25},{25,17},{2,10},{10... | collective-permute-start | bytes 393224 | tf_op jit(solution)/shard_map/ppermute | solution.py:344
  31.9 18.6 %collective-permute-start.17 = (bf16[2,128,512]{2,1,0:T(8,128)(2,1)S(1)}, bf16[2,128,512]{2,1,0:T(8,128)(2,1)S(1)}, u32[]{:S(2)}, u32[]{:S(2)}) collective-permute-start(bf16[2,128,512]{2,1,0:T(8,128)(2,1)S(1)} %get-tuple-element.98), channel_id=1, source_target_pairs={{0,8},{8,0},{16,24},{24,16},{1,9},{9,1},{17,25},{25,17},{2,10},{10... | collective-permute-start | bytes 786440 | tf_op jit(solution)/shard_map/ppermute | solution.py:344
  32.9 20.8 %collective-permute-start.18 = (bf16[2,128,512]{2,1,0:T(8,128)(2,1)S(1)}, bf16[2,128,512]{2,1,0:T(8,128)(2,1)S(1)}, u32[]{:S(2)}, u32[]{:S(2)}) collective-permute-start(bf16[2,128,512]{2,1,0:T(8,128)(2,1)S(1)} %get-tuple-element.99), channel_id=1, source_target_pairs={{0,16},{8,24},{16,0},{24,8},{1,17},{9,25},{17,1},{25,9},{2,18},{10... | collective-permute-start | bytes 786440 | tf_op jit(solution)/shard_map/ppermute | solution.py:344
  33.9 19.8 %collective-permute-start.19 = (bf16[2,128,512]{2,1,0:T(8,128)(2,1)S(1)}, bf16[2,128,512]{2,1,0:T(8,128)(2,1)S(1)}, u32[]{:S(2)}, u32[]{:S(2)}) collective-permute-start(bf16[2,128,512]{2,1,0:T(8,128)(2,1)S(1)} %get-tuple-element.100), channel_id=1, source_target_pairs={{0,24},{8,16},{16,8},{24,0},{1,25},{9,17},{17,9},{25,1},{2,26},{10... | collective-permute-start | bytes 786440 | tf_op jit(solution)/shard_map/ppermute | solution.py:344
  35.4 13.2 %collective-permute-start.8 = (bf16[2,128,256]{2,1,0:T(8,128)(2,1)S(1)}, bf16[2,128,256]{2,1,0:T(8,128)(2,1)S(1)}, u32[]{:S(2)}, u32[]{:S(2)}) collective-permute-start(bf16[2,128,256]{2,1,0:T(8,128)(2,1)S(1)} %get-tuple-element.87), channel_id=1, source_target_pairs={{0,16},{8,24},{16,0},{24,8},{1,17},{9,25},{17,1},{25,9},{2,18},{10... | collective-permute-start | bytes 393224 | tf_op jit(solution)/shard_map/ppermute | solution.py:344
  57.4 12.7 %collective-permute-start.20 = (bf16[128,512]{1,0:T(8,128)(2,1)S(1)}, bf16[128,512]{1,0:T(8,128)(2,1)S(1)}, u32[]{:S(2)}, u32[]{:S(2)}) collective-permute-start(bf16[128,512]{1,0:T(8,128)(2,1)S(1)} %get-tuple-element.102), channel_id=1, source_target_pairs={{0,1},{1,0},{2,3},{3,2},{4,5},{5,4},{6,7},{7,6},{8,9},{9,8},{10,11... | collective-permute-start | bytes 393224 | tf_op jit(solution)/shard_map/ppermute | solution.py:344
  57.7 13.2 %collective-permute-start.21 = (bf16[128,512]{1,0:T(8,128)(2,1)S(1)}, bf16[128,512]{1,0:T(8,128)(2,1)S(1)}, u32[]{:S(2)}, u32[]{:S(2)}) collective-permute-start(bf16[128,512]{1,0:T(8,128)(2,1)S(1)} %get-tuple-element.103), channel_id=1, source_target_pairs={{0,2},{1,3},{2,0},{3,1},{4,6},{5,7},{6,4},{7,5},{8,10},{9,11},{10,... | collective-permute-start | bytes 393224 | tf_op jit(solution)/shard_map/ppermute | solution.py:344
  69.3 19.0 %collective-permute-start.24 = (bf16[128,512]{1,0:T(8,128)(2,1)S(1)}, bf16[128,512]{1,0:T(8,128)(2,1)S(1)}, u32[]{:S(2)}, u32[]{:S(2)}) collective-permute-start(bf16[128,512]{1,0:T(8,128)(2,1)S(1)} %get-tuple-element.106), channel_id=1, source_target_pairs={{0,5},{1,4},{2,7},{3,6},{4,1},{5,0},{6,3},{7,2},{8,13},{9,12},{10,... | collective-permute-start | bytes 393224 | tf_op jit(solution)/shard_map/ppermute | solution.py:344
  70.1 18.2 %collective-permute-start.25 = (bf16[128,512]{1,0:T(8,128)(2,1)S(1)}, bf16[128,512]{1,0:T(8,128)(2,1)S(1)}, u32[]{:S(2)}, u32[]{:S(2)}) collective-permute-start(bf16[128,512]{1,0:T(8,128)(2,1)S(1)} %get-tuple-element.107), channel_id=1, source_target_pairs={{0,6},{1,7},{2,4},{3,5},{4,2},{5,3},{6,0},{7,1},{8,14},{9,15},{10,... | collective-permute-start | bytes 393224 | tf_op jit(solution)/shard_map/ppermute | solution.py:344
  70.8 17.9 %collective-permute-start.26 = (bf16[128,512]{1,0:T(8,128)(2,1)S(1)}, bf16[128,512]{1,0:T(8,128)(2,1)S(1)}, u32[]{:S(2)}, u32[]{:S(2)}) collective-permute-start(bf16[128,512]{1,0:T(8,128)(2,1)S(1)} %get-tuple-element.108), channel_id=1, source_target_pairs={{0,7},{1,6},{2,5},{3,4},{4,3},{5,2},{6,1},{7,0},{8,15},{9,14},{10,... | collective-permute-start | bytes 393224 | tf_op jit(solution)/shard_map/ppermute | solution.py:344
  77.4 17.3 %collective-permute-start.12 = (bf16[128,256]{1,0:T(8,128)(2,1)S(1)}, bf16[128,256]{1,0:T(8,128)(2,1)S(1)}, u32[]{:S(2)}, u32[]{:S(2)}) collective-permute-start(bf16[128,256]{1,0:T(8,128)(2,1)S(1)} %get-tuple-element.92), channel_id=1, source_target_pairs={{0,3},{1,2},{2,1},{3,0},{4,7},{5,6},{6,5},{7,4},{8,11},{9,10},{10,... | collective-permute-start | bytes 196616 | tf_op jit(solution)/shard_map/ppermute | solution.py:344
  77.5 22.0 %collective-permute-start.13 = (bf16[128,256]{1,0:T(8,128)(2,1)S(1)}, bf16[128,256]{1,0:T(8,128)(2,1)S(1)}, u32[]{:S(2)}, u32[]{:S(2)}) collective-permute-start(bf16[128,256]{1,0:T(8,128)(2,1)S(1)} %get-tuple-element.93), channel_id=1, source_target_pairs={{0,4},{1,5},{2,6},{3,7},{4,0},{5,1},{6,2},{7,3},{8,12},{9,13},{10,... | collective-permute-start | bytes 196616 | tf_op jit(solution)/shard_map/ppermute | solution.py:344
  88.3 13.3 %collective-permute-start.14 = (bf16[128,256]{1,0:T(8,128)(2,1)S(1)}, bf16[128,256]{1,0:T(8,128)(2,1)S(1)}, u32[]{:S(2)}, u32[]{:S(2)}) collective-permute-start(bf16[128,256]{1,0:T(8,128)(2,1)S(1)} %get-tuple-element.94), channel_id=1, source_target_pairs={{0,5},{1,4},{2,7},{3,6},{4,1},{5,0},{6,3},{7,2},{8,13},{9,12},{10,... | collective-permute-start | bytes 196616 | tf_op jit(solution)/shard_map/ppermute | solution.py:344
  88.3 13.3 %collective-permute-start.15 = (bf16[128,256]{1,0:T(8,128)(2,1)S(1)}, bf16[128,256]{1,0:T(8,128)(2,1)S(1)}, u32[]{:S(2)}, u32[]{:S(2)}) collective-permute-start(bf16[128,256]{1,0:T(8,128)(2,1)S(1)} %get-tuple-element.95), channel_id=1, source_target_pairs={{0,6},{1,7},{2,4},{3,5},{4,2},{5,3},{6,0},{7,1},{8,14},{9,15},{10,... | collective-permute-start | bytes 196616 | tf_op jit(solution)/shard_map/ppermute | solution.py:344
  88.8 12.8 %collective-permute-start.16 = (bf16[128,256]{1,0:T(8,128)(2,1)S(1)}, bf16[128,256]{1,0:T(8,128)(2,1)S(1)}, u32[]{:S(2)}, u32[]{:S(2)}) collective-permute-start(bf16[128,256]{1,0:T(8,128)(2,1)S(1)} %get-tuple-element.96), channel_id=1, source_target_pairs={{0,7},{1,6},{2,5},{3,4},{4,3},{5,2},{6,1},{7,0},{8,15},{9,14},{10,... | collective-permute-start | bytes 196616 | tf_op jit(solution)/shard_map/ppermute | solution.py:344
  110.4 13.9 %collective-permute-start.47 = (bf16[128,512]{1,0:T(8,128)(2,1)S(1)}, bf16[128,512]{1,0:T(8,128)(2,1)S(1)}, u32[]{:S(2)}, u32[]{:S(2)}) collective-permute-start(bf16[128,512]{1,0:T(8,128)(2,1)S(1)} %get-tuple-element.140), channel_id=1, source_target_pairs={{0,1},{1,0},{2,3},{3,2},{4,5},{5,4},{6,7},{7,6},{8,9},{9,8},{10,11... | collective-permute-start | bytes 393224 | tf_op jit(solution)/shard_map/ppermute | solution.py:344
  111.1 15.2 %collective-permute-start.48 = (bf16[128,512]{1,0:T(8,128)(2,1)S(1)}, bf16[128,512]{1,0:T(8,128)(2,1)S(1)}, u32[]{:S(2)}, u32[]{:S(2)}) collective-permute-start(bf16[128,512]{1,0:T(8,128)(2,1)S(1)} %get-tuple-element.141), channel_id=1, source_target_pairs={{0,2},{1,3},{2,0},{3,1},{4,6},{5,7},{6,4},{7,5},{8,10},{9,11},{10,... | collective-permute-start | bytes 393224 | tf_op jit(solution)/shard_map/ppermute | solution.py:344
  121.9 18.5 %collective-permute-start.50 = (bf16[128,512]{1,0:T(8,128)(2,1)S(1)}, bf16[128,512]{1,0:T(8,128)(2,1)S(1)}, u32[]{:S(2)}, u32[]{:S(2)}) collective-permute-start(bf16[128,512]{1,0:T(8,128)(2,1)S(1)} %get-tuple-element.143), channel_id=1, source_target_pairs={{0,4},{1,5},{2,6},{3,7},{4,0},{5,1},{6,2},{7,3},{8,12},{9,13},{10,... | collective-permute-start | bytes 393224 | tf_op jit(solution)/shard_map/ppermute | solution.py:344
  124.3 17.1 %collective-permute-start.51 = (bf16[128,512]{1,0:T(8,128)(2,1)S(1)}, bf16[128,512]{1,0:T(8,128)(2,1)S(1)}, u32[]{:S(2)}, u32[]{:S(2)}) collective-permute-start(bf16[128,512]{1,0:T(8,128)(2,1)S(1)} %get-tuple-element.144), channel_id=1, source_target_pairs={{0,5},{1,4},{2,7},{3,6},{4,1},{5,0},{6,3},{7,2},{8,13},{9,12},{10,... | collective-permute-start | bytes 393224 | tf_op jit(solution)/shard_map/ppermute | solution.py:344
  124.3 18.5 %collective-permute-start.52 = (bf16[128,512]{1,0:T(8,128)(2,1)S(1)}, bf16[128,512]{1,0:T(8,128)(2,1)S(1)}, u32[]{:S(2)}, u32[]{:S(2)}) collective-permute-start(bf16[128,512]{1,0:T(8,128)(2,1)S(1)} %get-tuple-element.145), channel_id=1, source_target_pairs={{0,6},{1,7},{2,4},{3,5},{4,2},{5,3},{6,0},{7,1},{8,14},{9,15},{10,... | collective-permute-start | bytes 393224 | tf_op jit(solution)/shard_map/ppermute | solution.py:344
  126.2 19.2 %collective-permute-start.53 = (bf16[128,512]{1,0:T(8,128)(2,1)S(1)}, bf16[128,512]{1,0:T(8,128)(2,1)S(1)}, u32[]{:S(2)}, u32[]{:S(2)}) collective-permute-start(bf16[128,512]{1,0:T(8,128)(2,1)S(1)} %get-tuple-element.146), channel_id=1, source_target_pairs={{0,7},{1,6},{2,5},{3,4},{4,3},{5,2},{6,1},{7,0},{8,15},{9,14},{10,... | collective-permute-start | bytes 393224 | tf_op jit(solution)/shard_map/ppermute | solution.py:344
  128.1 21.2 %collective-permute-start.38 = (bf16[128,256]{1,0:T(8,128)(2,1)S(1)}, bf16[128,256]{1,0:T(8,128)(2,1)S(1)}, u32[]{:S(2)}, u32[]{:S(2)}) collective-permute-start(bf16[128,256]{1,0:T(8,128)(2,1)S(1)} %get-tuple-element.129), channel_id=1, source_target_pairs={{0,2},{1,3},{2,0},{3,1},{4,6},{5,7},{6,4},{7,5},{8,10},{9,11},{10,... | collective-permute-start | bytes 196616 | tf_op jit(solution)/shard_map/ppermute | solution.py:344
  141.4 12.9 %collective-permute-start.40 = (bf16[128,256]{1,0:T(8,128)(2,1)S(1)}, bf16[128,256]{1,0:T(8,128)(2,1)S(1)}, u32[]{:S(2)}, u32[]{:S(2)}) collective-permute-start(bf16[128,256]{1,0:T(8,128)(2,1)S(1)} %get-tuple-element.131), channel_id=1, source_target_pairs={{0,4},{1,5},{2,6},{3,7},{4,0},{5,1},{6,2},{7,3},{8,12},{9,13},{10,... | collective-permute-start | bytes 196616 | tf_op jit(solution)/shard_map/ppermute | solution.py:344
  149.3 13.8 %collective-permute-start.43 = (bf16[128,256]{1,0:T(8,128)(2,1)S(1)}, bf16[128,256]{1,0:T(8,128)(2,1)S(1)}, u32[]{:S(2)}, u32[]{:S(2)}) collective-permute-start(bf16[128,256]{1,0:T(8,128)(2,1)S(1)} %get-tuple-element.134), channel_id=1, source_target_pairs={{0,7},{1,6},{2,5},{3,4},{4,3},{5,2},{6,1},{7,0},{8,15},{9,14},{10,... | collective-permute-start | bytes 196616 | tf_op jit(solution)/shard_map/ppermute | solution.py:344
  163.9 21.5 %collective-permute-start.44 = (bf16[2,128,256]{2,1,0:T(8,128)(2,1)S(1)}, bf16[2,128,256]{2,1,0:T(8,128)(2,1)S(1)}, u32[]{:S(2)}, u32[]{:S(2)}) collective-permute-start(bf16[2,128,256]{2,1,0:T(8,128)(2,1)S(1)} %get-tuple-element.136), channel_id=1, source_target_pairs={{0,8},{8,0},{16,24},{24,16},{1,9},{9,1},{17,25},{25,17},{2,10},{10... | collective-permute-start | bytes 393224 | tf_op jit(solution)/shard_map/ppermute | solution.py:344
  164.5 20.9 %collective-permute-start.45 = (bf16[2,128,256]{2,1,0:T(8,128)(2,1)S(1)}, bf16[2,128,256]{2,1,0:T(8,128)(2,1)S(1)}, u32[]{:S(2)}, u32[]{:S(2)}) collective-permute-start(bf16[2,128,256]{2,1,0:T(8,128)(2,1)S(1)} %get-tuple-element.137), channel_id=1, source_target_pairs={{0,16},{8,24},{16,0},{24,8},{1,17},{9,25},{17,1},{25,9},{2,18},{10... | collective-permute-start | bytes 393224 | tf_op jit(solution)/shard_map/ppermute | solution.py:344
  165.6 19.8 %collective-permute-start.46 = (bf16[2,128,256]{2,1,0:T(8,128)(2,1)S(1)}, bf16[2,128,256]{2,1,0:T(8,128)(2,1)S(1)}, u32[]{:S(2)}, u32[]{:S(2)}) collective-permute-start(bf16[2,128,256]{2,1,0:T(8,128)(2,1)S(1)} %get-tuple-element.138), channel_id=1, source_target_pairs={{0,24},{8,16},{16,8},{24,0},{1,25},{9,17},{17,9},{25,1},{2,26},{10... | collective-permute-start | bytes 393224 | tf_op jit(solution)/shard_map/ppermute | solution.py:344
  167.5 16.1 %collective-permute-start.55 = (bf16[2,128,512]{2,1,0:T(8,128)(2,1)S(1)}, bf16[2,128,512]{2,1,0:T(8,128)(2,1)S(1)}, u32[]{:S(2)}, u32[]{:S(2)}) collective-permute-start(bf16[2,128,512]{2,1,0:T(8,128)(2,1)S(1)} %get-tuple-element.149), channel_id=1, source_target_pairs={{0,16},{8,24},{16,0},{24,8},{1,17},{9,25},{17,1},{25,9},{2,18},{10... | collective-permute-start | bytes 786440 | tf_op jit(solution)/shard_map/ppermute | solution.py:344
  168.1 15.5 %collective-permute-start.56 = (bf16[2,128,512]{2,1,0:T(8,128)(2,1)S(1)}, bf16[2,128,512]{2,1,0:T(8,128)(2,1)S(1)}, u32[]{:S(2)}, u32[]{:S(2)}) collective-permute-start(bf16[2,128,512]{2,1,0:T(8,128)(2,1)S(1)} %get-tuple-element.150), channel_id=1, source_target_pairs={{0,24},{8,16},{16,8},{24,0},{1,25},{9,17},{17,9},{25,1},{2,26},{10... | collective-permute-start | bytes 786440 | tf_op jit(solution)/shard_map/ppermute | solution.py:344
  (41 other events, 516.2 us)
